TPU v7x, 32 devices: a whole 2x2x4 slice. The times are simulated.
32 devices in a mesh: feed: 4 (over y, core), tm: 8 (over z, x).
Axes of the slice: x: 2, y: 2, z: 4, core: 2. Of those that a mesh axis runs over, the one named last changes fastest.
Arguments:
- tod: bfloat16 [8192, 50, 256], P(('feed', 'tm')), may hold values from -6 to 6
- pixels: int32 [8192, 50], P(('feed', 'tm')), may hold values from 0 to 31
- block_slots: int32 [8192], P(('feed', 'tm')), may hold values from 0 to 7, as said below
- tile_lists: int32 [32, 8, 1], P(('feed', 'tm')), may hold values from -1 to 63, as said below
- tile_place: int32 [64], replicated, may hold values from 0 to 63, as said below
- prior: float32 [256], replicated, may hold values from 0.5 to 4
Outputs:
- drift_levels: float32 [8192, 256], P(('feed', 'tm'))
- leftover_error: float32 [8192, 256], P(('feed', 'tm'))
- destriped_result_map: float32 [64, 32, 256], P('tm', None, 'feed')
Inputs may be any that keep to these rules, and one draw needn't show every extreme that they name: tile_lists[g, o, s] is -1 or a tile whose tile_place // 8 equals o; the live entries of one device are distinct; entries 0 and 7 of each device's flattened list are live; some tiles are named by no list. block_slots[b] names a live entry of the flattened list of the device that holds baseline b. tile_place is a permutation of the tiles; place p is stored by tm index p // 8 in its row p % 8.
All inputs are finite; a program needn't handle non-finite values.
Results may differ from a plain program's by a relative error of at most 0.0013.
Values sent between devices are 32-bit elements; how exact they have to be, the bound alone decides.
No kernel may reach another device: no remote copies, remote signals or barrier semaphores. Data moves between devices by JAX's collectives and lax.ppermute only.
A program may use at most 64 MiB of HBM per device.

v0:
```python
import jax
import jax.numpy as jnp
from jax import lax
from jax.sharding import PartitionSpec as P

CELLS_IN_PATCH = 32
ITERS = 2


def local(tod, pixels, block_slots, tile_lists, tile_place, prior):
    highest = lax.Precision.HIGHEST
    tm_count = lax.axis_size("tm")
    feed_count = lax.axis_size("feed")
    slot_count = tile_lists.shape[1] * tile_lists.shape[2]
    tile_total = tile_place.shape[0]
    rows_owned = tile_total // tm_count
    owner_index = lax.axis_index("tm")
    block_count = tod.shape[0]
    sample_count = tod.shape[1]
    channels = tod.shape[2]
    share_width = channels // feed_count
    pix_match = pixels[:, :, None] == jnp.arange(CELLS_IN_PATCH, dtype=jnp.int32)[None, None, :]
    hit_blocks = jnp.sum(pix_match.astype(jnp.float32), axis=1)
    slot_hot = (block_slots[:, None] == jnp.arange(slot_count, dtype=jnp.int32)[None, :]).astype(
        jnp.float32
    )
    weights = (slot_hot[:, :, None] * hit_blocks[:, None, :]).reshape(
        block_count, slot_count * CELLS_IN_PATCH
    )
    hit_slots = jnp.sum(weights, axis=0).reshape(slot_count, CELLS_IN_PATCH)
    my_list = tile_lists.reshape(slot_count)
    recv_hits, recv_tiles = (
        lax.all_to_all(hit_slots, "tm", split_axis=0, concat_axis=0, tiled=True),
        lax.all_to_all(my_list, "tm", split_axis=0, concat_axis=0, tiled=True),
    )
    matches = recv_tiles[:, None] == jnp.arange(tile_total, dtype=jnp.int32)[None, :]
    recv_place = jnp.sum(jnp.where(matches, tile_place[None, :] + 1, 0), axis=1) - 1
    local_rows = owner_index * rows_owned + jnp.arange(rows_owned, dtype=jnp.int32)
    select = (local_rows[:, None] == recv_place[None, :]).astype(jnp.float32)
    owned_hits = jnp.dot(select, recv_hits, precision=highest)
    hits = lax.psum(owned_hits, "feed")
    inverse = 1.0 / jnp.maximum(hits, 1.0)

    def averaged_patch_lines(slot_parts):
        received = lax.all_to_all(slot_parts, "tm", split_axis=0, concat_axis=0, tiled=True)
        owned_sum = jnp.einsum("lk,kpc->lpc", select, received, precision=highest)
        summed = lax.psum(owned_sum, "feed")
        return summed * inverse[:, :, None]

    def project(slot_parts, sample_sums):
        sky_tiles = averaged_patch_lines(slot_parts)
        outgoing = jnp.einsum("lk,lpc->kpc", select, sky_tiles, precision=highest)
        returned = lax.all_to_all(outgoing, "tm", split_axis=0, concat_axis=0, tiled=True)
        flat_tiles = returned.reshape(slot_count * CELLS_IN_PATCH, channels)
        mapped = jnp.dot(weights, flat_tiles, precision=highest)
        return sample_sums - mapped

    def unrolled_drift_levels(values):
        parts_flat = jnp.einsum("bq,bc->qc", weights, values, precision=highest)
        return parts_flat.reshape(slot_count, CELLS_IN_PATCH, channels)

    def squares(values):
        return lax.psum(jnp.sum(values * values), ("feed", "tm"))

    pix_hot = pix_match.astype(jnp.bfloat16)
    per_block = jnp.einsum("bsp,bsc->bpc", pix_hot, tod, preferred_element_type=jnp.float32)
    observation_segments = jnp.einsum("bk,bpc->kpc", slot_hot, per_block, precision=highest)
    data_sums = jnp.sum(per_block, axis=1)
    system_target = project(observation_segments, data_sums)
    drift_levels = jnp.zeros_like(system_target)
    leftover_error = system_target
    descent_direction = system_target
    norm_now = squares(leftover_error)
    for number in range(ITERS):
        image = (
            project(unrolled_drift_levels(descent_direction), sample_count * descent_direction)
            + prior[None, :] * descent_direction
        )
        update_factor = norm_now / lax.psum(jnp.sum(descent_direction * image), ("feed", "tm"))
        drift_levels = drift_levels + update_factor * descent_direction
        leftover_error = leftover_error - update_factor * image
        norm_next = squares(leftover_error)
        descent_direction = leftover_error + norm_next / norm_now * descent_direction
        norm_now = norm_next
    converged_patch_lines = averaged_patch_lines(
        observation_segments - unrolled_drift_levels(drift_levels)
    )
    destriped_result_map = lax.dynamic_slice_in_dim(
        converged_patch_lines, lax.axis_index("feed") * share_width, share_width, 2
    )
    return (drift_levels, leftover_error, destriped_result_map)


def solution(mesh):
    return jax.shard_map(
        local,
        mesh=mesh,
        in_specs=(
            P(("feed", "tm"), None, None),
            P(("feed", "tm"), None),
            P(("feed", "tm")),
            P(("feed", "tm"), None, None),
            P(),
            P(),
        ),
        out_specs=(P(("feed", "tm"), None), P(("feed", "tm"), None), P("tm", None, "feed")),
        check_vma=False,
    )
```

profile of v0, /device:TPU:0, one launch (start us, length us, event | category | flops | bytes accessed | tf_op | source)
XLA Modules:
  0.0 404.3 jit_solution(7255400728901228236)
XLA Ops:
  7.2 1.3 copy.88
  8.5 7.3 %all-to-all-start = ((s32[8,1,1]{2,1,0:T(1,128)}), s32[8,1,1]{2,1,0:T(1,128)S(1)}, u32[]{:S(2)}, u32[]{:S(2)}) async-start(s32[8,1,1]{2,1,0:T(1,128)} %copy.88), calls=%async_computation | async-start | bytes 8192 | tf_op jit(solution)/shard_map/all_to_all | solution.py:34
  16.7 1.2 convert_reduce_fusion
  17.9 7.7 %fusion.54 = (f32[256,256]{1,0:T(8,128)S(1)}, f32[256,32,256]{2,1,0:T(8,128)S(1)}) fusion(bf16[256,50,256]{2,0,1:T(8,128)(2,1)} %param.6, s32[256,50]{1,0:T(8,128)S(1)} %copy.85), kind=kOutput, calls=%fused_computation.78 | convolution fusion | flops 212156416 | bytes 15255552 | tf_op jit(solution)/shard_map/bsp,bsc->bpc/dot_general | solution.py:66
  25.6 7.7 %fusion = f32[8,32,256]{2,0,1:T(8,128)S(1)} fusion(f32[256,32,256]{2,1,0:T(8,128)S(1)} %get-tuple-element.30, s32[256]{0:T(256)S(1)} %copy-done.1), kind=kOutput, calls=%fused_computation | convolution fusion | flops 201328640 | bytes 8651776 | tf_op jit(solution)/shard_map/bk,bpc->kpc/dot_general | solution.py:67
  34.1 6.0 %all-to-all-start.2 = ((f32[8,1,32]{2,1,0:T(1,128)}), f32[8,1,32]{2,1,0:T(1,128)S(1)}, u32[]{:S(2)}, u32[]{:S(2)}) async-start(f32[8,1,32]{2,1,0:T(1,128)} %bitcast.4), calls=%async_computation.2 | async-start | bytes 8192 | tf_op jit(solution)/shard_map/all_to_all | solution.py:33
  41.1 5.4 %all-to-all-done.2 = f32[8,1,32]{2,1,0:T(1,128)S(1)} async-done(((f32[8,1,32]{2,1,0:T(1,128)}), f32[8,1,32]{2,1,0:T(1,128)S(1)}, u32[]{:S(2)}, u32[]{:S(2)}) %all-to-all-start.2) | async-done | bytes 1056 | tf_op jit(solution)/shard_map/all_to_all | solution.py:33
  46.5 3.4 all-to-all-start.1
  50.4 5.9 %psum.64 = f32[8,32]{1,0:T(8,128)S(1)} all-reduce(f32[8,32]{1,0:T(8,128)S(1)} %fusion.49), channel_id=1, replica_groups=mesh['feed'=4,'tm'=8] {'feed'}, use_global_device_ids=true, to_apply=%region_5.6 | all-reduce | flops 256 | bytes 2048 | tf_op jit(solution)/shard_map/psum | solution.py:41
  56.3 1.8 all-to-all-done.1
  58.1 1.1 fusion.25
  59.4 31.9 %all-reduce.6.cloned.1.call-done = f32[8,32,256]{2,0,1:T(8,128)} async-done(((f32[8,32,256]{2,0,1:T(8,128)}), f32[8,32,256]{2,0,1:T(8,128)}) %all-reduce.6.cloned.1.call-update) | async-done | bytes 262160 | tf_op jit(solution)/shard_map/psum | solution.py:47
  91.2 1.3 fusion.31
  92.7 13.5 %all_to_all.56 = f32[8,32,256]{2,1,0:T(8,128)S(1)} all-to-all(f32[8,32,256]{2,1,0:T(8,128)S(1)} %copy.94), channel_id=1, replica_groups=mesh['feed'=4,'tm'=8] {'tm'}, dimensions={0} | all-to-all | bytes 524288 | tf_op jit(solution)/shard_map/all_to_all | solution.py:53
  107.2 11.1 %all_to_all.57 = f32[8,32,256]{2,1,0:T(8,128)S(1)} all-to-all(f32[8,32,256]{2,1,0:T(8,128)S(1)} %fusion.16), channel_id=1, replica_groups=mesh['feed'=4,'tm'=8] {'tm'}, dimensions={0} | all-to-all | bytes 524288 | tf_op jit(solution)/shard_map/all_to_all | solution.py:45
  118.3 1.1 fusion.23
  119.5 31.2 %all-reduce.8.cloned.1.call-done = f32[8,32,256]{2,0,1:T(8,128)} async-done(((f32[8,32,256]{2,0,1:T(8,128)}), f32[8,32,256]{2,0,1:T(8,128)}) %all-reduce.8.cloned.1.call-update) | async-done | bytes 262160 | tf_op jit(solution)/shard_map/psum | solution.py:47
  150.8 1.3 fusion.29
  152.2 13.5 %all_to_all.58 = f32[8,32,256]{2,1,0:T(8,128)S(1)} all-to-all(f32[8,32,256]{2,1,0:T(8,128)S(1)} %copy.97), channel_id=1, replica_groups=mesh['feed'=4,'tm'=8] {'tm'}, dimensions={0} | all-to-all | bytes 524288 | tf_op jit(solution)/shard_map/all_to_all | solution.py:53
  165.7 1.2 multiply_reduce_fusion.3
  167.0 38.0 %all-reduce = (f32[]{:T(128)}, f32[]{:T(128)}) all-reduce(f32[]{:T(128)} %get-tuple-element.22, f32[]{:T(128)} %get-tuple-element.21), channel_id=1, replica_groups=mesh['feed'=4,'tm'=8] {'feed','tm'}, use_global_device_ids=true, to_apply=%region_7.8 | all-reduce | flops 2 | bytes 16 | tf_op jit(solution)/shard_map/psum | solution.py:63
  207.0 41.4 %psum.68 = f32[]{:T(128)} all-reduce(f32[]{:T(128)} %multiply_reduce_fusion.2), channel_id=1, replica_groups=mesh['feed'=4,'tm'=8] {'feed','tm'}, use_global_device_ids=true, to_apply=%region_12.13 | all-reduce | flops 1 | bytes 8 | tf_op jit(solution)/shard_map/psum | solution.py:63
  250.2 12.5 %all_to_all.59 = f32[8,32,256]{2,1,0:T(8,128)S(1)} all-to-all(f32[8,32,256]{2,1,0:T(8,128)S(1)} %fusion.14), channel_id=1, replica_groups=mesh['feed'=4,'tm'=8] {'tm'}, dimensions={0} | all-to-all | bytes 524288 | tf_op jit(solution)/shard_map/all_to_all | solution.py:45
  262.7 1.1 fusion.21
  263.9 30.5 %all-reduce.10.cloned.1.call-done = f32[8,32,256]{2,0,1:T(8,128)} async-done(((f32[8,32,256]{2,0,1:T(8,128)}), f32[8,32,256]{2,0,1:T(8,128)}) %all-reduce.10.cloned.1.call-update) | async-done | bytes 262160 | tf_op jit(solution)/shard_map/psum | solution.py:47
  294.4 1.3 fusion.27
  295.9 13.5 %all_to_all.60 = f32[8,32,256]{2,1,0:T(8,128)S(1)} all-to-all(f32[8,32,256]{2,1,0:T(8,128)S(1)} %copy.100), channel_id=1, replica_groups=mesh['feed'=4,'tm'=8] {'tm'}, dimensions={0} | all-to-all | bytes 524288 | tf_op jit(solution)/shard_map/all_to_all | solution.py:53
  309.4 1.2 multiply_reduce_fusion.1
  310.6 37.9 %psum.70 = f32[]{:T(128)} all-reduce(f32[]{:T(128)} %get-tuple-element.32), channel_id=1, replica_groups=mesh['feed'=4,'tm'=8] {'feed','tm'}, use_global_device_ids=true, to_apply=%region_15.16 | all-reduce | flops 1 | bytes 8 | tf_op jit(solution)/shard_map/psum | solution.py:79
  351.3 13.1 %all_to_all.61 = f32[8,32,256]{2,1,0:T(8,128)S(1)} all-to-all(f32[8,32,256]{2,1,0:T(8,128)S(1)} %copy.102), channel_id=1, replica_groups=mesh['feed'=4,'tm'=8] {'tm'}, dimensions={0} | all-to-all | bytes 524288 | tf_op jit(solution)/shard_map/all_to_all | solution.py:45
  364.3 1.1 fusion.18
  365.5 30.6 %all-reduce.12.cloned.1.call-done = f32[8,32,256]{2,0,1:T(8,128)} async-done(((f32[8,32,256]{2,0,1:T(8,128)}), f32[8,32,256]{2,0,1:T(8,128)}) %all-reduce.12.cloned.1.call-update) | async-done | bytes 262160 | tf_op jit(solution)/shard_map/psum | solution.py:47
  (42 shorter events, 8.8 us)
Async XLA Ops:
  8.5 25.6 %all-to-all-start = ((s32[8,1,1]{2,1,0:T(1,128)}), s32[8,1,1]{2,1,0:T(1,128)S(1)}, u32[]{:S(2)}, u32[]{:S(2)}) async-start(s32[8,1,1]{2,1,0:T(1,128)} %copy.88), calls=%async_computation | async-start | bytes 8192 | tf_op jit(solution)/shard_map/all_to_all | solution.py:34
  17.8 7.8 %copy-start.1 = (s32[256]{0:T(256)S(1)}, s32[256]{0:T(256)}, u32[]{:S(2)}) copy-start(s32[256]{0:T(256)} %param.8) | copy-start | bytes 3076
  25.6 14.5 %copy-start.3 = (s32[64]{0:T(128)S(1)}, s32[64]{0:T(128)}, u32[]{:S(2)}) copy-start(s32[64]{0:T(128)} %param.10) | copy-start | bytes 772
  25.6 140.1 %copy-start.2 = (f32[256]{0:T(256)S(1)}, f32[256]{0:T(256)}, u32[]{:S(2)}) copy-start(f32[256]{0:T(256)} %param.11) | copy-start | bytes 3076
  34.1 12.4 %all-to-all-start.2 = ((f32[8,1,32]{2,1,0:T(1,128)}), f32[8,1,32]{2,1,0:T(1,128)S(1)}, u32[]{:S(2)}, u32[]{:S(2)}) async-start(f32[8,1,32]{2,1,0:T(1,128)} %bitcast.4), calls=%async_computation.2 | async-start | bytes 8192 | tf_op jit(solution)/shard_map/all_to_all | solution.py:33
  46.5 11.6 %all-to-all-start.1 = ((f32[8,32,256]{2,1,0:T(8,128)}), f32[8,32,256]{2,1,0:T(8,128)S(1)}, u32[]{:S(2)}, u32[]{:S(2)}) async-start(f32[8,32,256]{2,1,0:T(8,128)} %copy.90), calls=%async_computation.1 | async-start | bytes 524288 | tf_op jit(solution)/shard_map/all_to_all | solution.py:45
  49.9 41.3 %all-reduce.6.cloned.1.call-start = ((), (), s32[]{:S(2)}) async-start(), calls=%async_computation.9 | async-start | bytes 524288 | tf_op jit(solution)/shard_map/psum | solution.py:47
  59.2 91.5 %all-reduce.8.cloned.1.call-start = ((), (), s32[]{:S(2)}) async-start(), calls=%async_computation.10 | async-start | bytes 524288 | tf_op jit(solution)/shard_map/psum | solution.py:47
  119.5 174.9 %all-reduce.10.cloned.1.call-start = ((), (), s32[]{:S(2)}) async-start(), calls=%async_computation.11 | async-start | bytes 524288 | tf_op jit(solution)/shard_map/psum | solution.py:47
  263.8 132.2 %all-reduce.12.cloned.1.call-start = ((), (), s32[]{:S(2)}) async-start(), calls=%async_computation.12 | async-start | bytes 524288 | tf_op jit(solution)/shard_map/psum | solution.py:47
  350.7 47.1 %copy-start = (f32[256,256]{1,0:T(8,128)}, f32[256,256]{1,0:T(8,128)S(1)}, u32[]{:S(2)}) copy-start(f32[256,256]{1,0:T(8,128)S(1)} %get-tuple-element.26) | copy-start | bytes 786436
Sparse Core Ops, SparseCore 0:
  59.4 31.8 all-reduce.5
  119.6 31.1 all-reduce.7
  264.0 30.4 all-reduce.9
  365.6 30.4 all-reduce.11
where the time goes:
time: 405 us; the launch traced here: 404 us
  blocking collectives  201 us (50%)
  waiting for transfers between devices  131 us (32%)
  matrix products  28.3 us (7%)
  between operations  18 us (4%)
  starting transfers between devices  16.9 us (4%)
  other arithmetic  4.82 us (1%)
  local copies, waits for them, and re-layouts  4.22 us (1%)
    psum x4, waiting for transfers between devices, averaged_patch_lines(): summed = lax.psum(owned_sum, 'feed')  124 us
    psum x2, blocking collectives, squares(): return lax.psum(jnp.sum(values * values), ('feed', 'tm'))  79.4 us
    all_to_all x3, blocking collectives, project(): lax.all_to_all(outgoing, 'tm', split_axis=0, concat_axis=0, tiled=True)  40.6 us
    psum x1, blocking collectives, local(): lax.psum(jnp.sum(descent_direction * image), ('feed', 'tm'))  37.9 us
    all_to_all x3, blocking collectives, averaged_patch_lines(): lax.all_to_all(slot_parts, 'tm', split_axis=0, concat_axis=0, tiled=True)  36.8 us
  transfers between devices with their start and end apart: 7, of which 6 were waited for; matrix products, arithmetic and copies ran while one was open for 5% of the time, Pallas kernels for 0%

commit v1 on v0

v1 whole, which is shorter than its diff:
```python
import jax
import jax.numpy as jnp
from jax import lax
from jax.experimental import pallas as pl
from jax.experimental.pallas import tpu as pltpu
from jax.sharding import PartitionSpec as P

CELLS = 32
EXACT = lax.Precision.HIGHEST
f32 = jnp.float32
bf16 = jnp.bfloat16


def split3(value):
    high = value.astype(bf16)
    rest = value - high.astype(f32)
    mid = rest.astype(bf16)
    low = (rest - mid.astype(f32)).astype(bf16)
    return high, mid, low


def counted(counts, value):
    out = None
    for part in split3(value):
        term = jnp.dot(counts, part, preferred_element_type=f32)
        out = term if out is None else out + term
    return out


def shift_of(prior):
    return jnp.sum(prior, axis=1, keepdims=True) * (1.0 / prior.shape[1])


def bin_kernel(
    list_ref, place_ref, slot_ref, pix_ref, tod_ref,
    pay_ref, sums_ref, w_ref, power_ref,
    t_acc, s_acc, wt_acc, g_scr, v_scr,
    *, slots, feeds, rows_owned, step_samples,
):
    step = pl.program_id(0)
    blocks = slot_ref.shape[1]
    cells = slots * CELLS
    lanes = pay_ref.shape[2]
    width = lanes // 2
    base = slot_ref[...] * CELLS
    row_id = lax.broadcasted_iota(jnp.int32, (cells, blocks), 0)
    hots = []
    count = None
    total = None
    for j in range(step_samples):
        cell = base + pix_ref[pl.ds(step * step_samples + j, 1), :]
        hot = (row_id == cell).astype(f32)
        count = hot if count is None else count + hot
        hots.append(hot.astype(bf16))
        now = tod_ref[j].astype(f32)
        total = now if total is None else total + now
    hot_all = jnp.concatenate(hots, axis=1)
    tod_all = tod_ref[...].reshape(step_samples * blocks, tod_ref.shape[2])
    binned = jnp.dot(hot_all, tod_all, preferred_element_type=f32)

    @pl.when(step == 0)
    def _():
        t_acc[...] = binned
        s_acc[...] = total
        wt_acc[...] = count

    @pl.when(step > 0)
    def _():
        t_acc[...] += binned
        s_acc[...] += total
        wt_acc[...] += count

    @pl.when(step == pl.num_programs(0) - 1)
    def _():
        sums = s_acc[...]
        wt = wt_acc[...].astype(bf16)
        sums_ref[...] = sums
        w_ref[...] = wt_acc[...].T.astype(bf16)
        power_ref[...] = jnp.sum(sums * sums, axis=0, keepdims=True)
        v_scr[...] = counted(wt, sums)
        g_scr[...] = lax.dot_general(wt, wt, (((1,), (1,)), ((), ())), preferred_element_type=f32)
        nb = lanes // CELLS
        rb = CELLS // nb
        sub = lax.broadcasted_iota(jnp.int32, (rb, lanes), 0)
        lane = lax.broadcasted_iota(jnp.int32, (rb, lanes), 1)
        mark = (sub == rb - 1) & (lane == (nb - 1) * CELLS)
        for k in range(slots):
            q0 = k * CELLS
            pack = jnp.concatenate(
                [g_scr[q0 + rb * i:q0 + rb * (i + 1), q0:q0 + CELLS] for i in range(nb)], axis=1
            )
            tile = list_ref[k]
            row = jnp.where(tile >= 0, lax.rem(place_ref[jnp.maximum(tile, 0)], rows_owned), -1)
            pack = jnp.where(mark, row.astype(f32), pack)
            for f in range(feeds):
                d = f * slots + k
                pay_ref[d, 0:CELLS, :] = jnp.concatenate(
                    [
                        t_acc[q0:q0 + CELLS, f * width:(f + 1) * width],
                        v_scr[q0:q0 + CELLS, f * width:(f + 1) * width],
                    ],
                    axis=1,
                )
                pay_ref[d, CELLS:CELLS + rb, :] = pack


def expand(gram_ref, k, pack, nb, rb):
    for i in range(nb):
        gram_ref[k * CELLS + rb * i:k * CELLS + rb * (i + 1), k * CELLS:(k + 1) * CELLS] = (
            pack[:, i * CELLS:(i + 1) * CELLS]
        )


def owner_kernel(
    feed_ref, recv_ref, prior_ref, power_ref,
    pay_ref, map_ref,
    acc_ref, gram_ref, pair_ref,
    *, feeds, rows_owned, samples,
):
    sources, rows, lanes = recv_ref.shape
    width = lanes // 2
    nb = lanes // CELLS
    rb = CELLS // nb
    tiles = rows // 8
    mark_row = CELLS + rb - 1
    mark_lane = (nb - 1) * CELLS

    def gather(d, accs):
        index = jnp.broadcast_to(recv_ref[d, mark_row:mark_row + 1, mark_lane:mark_lane + 1], (8, lanes))
        values = [recv_ref[d, 8 * j:8 * j + 8, :] for j in range(tiles)]
        out = []
        for r in range(rows_owned):
            hit = index == float(r)
            for j in range(tiles):
                out.append(accs[r * tiles + j] + jnp.where(hit, values[j], 0.0))
        return tuple(out)

    zero = jnp.zeros((8, lanes), f32)
    accs = lax.fori_loop(0, sources, gather, (zero,) * (rows_owned * tiles), unroll=4)
    for r in range(rows_owned):
        for j in range(tiles):
            acc_ref[r, 8 * j:8 * j + 8, :] = accs[r * tiles + j]
    gram_ref[...] = jnp.zeros(gram_ref.shape, f32)
    sub = lax.broadcasted_iota(jnp.int32, (rb, lanes), 0)
    lane = lax.broadcasted_iota(jnp.int32, (rb, lanes), 1)
    mark = (sub == rb - 1) & (lane == mark_lane)
    packs = []
    for r in range(rows_owned):
        pack = acc_ref[r, CELLS:CELLS + rb, :]
        pack = jnp.where(mark, pack[0:1, CELLS - 1:CELLS], pack)
        packs.append(pack)
        expand(gram_ref, r, pack, nb, rb)
    gram = gram_ref[...]
    hits = jnp.sum(gram, axis=1, keepdims=True) / float(samples)
    inverse = 1.0 / jnp.maximum(hits, 1.0)
    both = jnp.concatenate([acc_ref[r, 0:CELLS, :] for r in range(rows_owned)], axis=0)
    t_sum = both[:, 0:width]
    v_sum = both[:, width:lanes]
    prior = prior_ref[...]
    offset = prior - shift_of(prior)
    feed = feed_ref[0]
    mine = offset[:, 0:width]
    for f in range(1, feeds):
        mine = jnp.where(feed == f, offset[:, f * width:(f + 1) * width], mine)
    y0 = t_sum * inverse
    u0 = v_sum - jnp.dot(gram, y0, precision=EXACT, preferred_element_type=f32)
    y1 = u0 * inverse
    uz = mine * u0 - jnp.dot(gram, y1, precision=EXACT, preferred_element_type=f32)
    y2 = uz * inverse
    map_ref[0] = y0
    map_ref[1] = y1
    map_ref[2] = y2
    rr = -jnp.sum(y0 * (v_sum + u0), axis=0, keepdims=True)
    cross = jnp.sum(u0 * y1, axis=0, keepdims=True)
    zz = mine * mine * rr - jnp.sum(y1 * (mine * u0 + uz), axis=0, keepdims=True)
    zw = mine * zz - jnp.sum(uz * y2, axis=0, keepdims=True)
    rz = mine * rr - cross
    power = power_ref[...]
    parts = []
    for own in (rr, rz, zz, zw):
        for f in range(feeds):
            own = own + power[:, f * width:(f + 1) * width]
        parts.append(own)
        power = power * offset
    scal0 = jnp.concatenate(parts[0:2], axis=1)
    scal1 = jnp.concatenate(parts[2:4], axis=1)
    pair_ref[...] = jnp.concatenate([y0, y1], axis=1)
    share = rb // feeds
    fill = jnp.zeros((rows - CELLS - share - 2, lanes), f32)
    tails = []
    for r in range(rows_owned):
        quarter = packs[r][0:share]
        for f in range(1, feeds):
            quarter = jnp.where(feed == f, packs[r][f * share:(f + 1) * share], quarter)
        tails.append(jnp.concatenate([quarter, scal0, scal1, fill], axis=0))

    def scatter(d, carry):
        index = jnp.broadcast_to(recv_ref[d, mark_row:mark_row + 1, mark_lane:mark_lane + 1], (8, lanes))
        hits_r = [index == float(r) for r in range(rows_owned)]
        for j in range(CELLS // 8):
            v = jnp.zeros((8, lanes), f32)
            for r in range(rows_owned):
                v = jnp.where(hits_r[r], pair_ref[r * CELLS + 8 * j:r * CELLS + 8 * j + 8, :], v)
            pay_ref[d, 8 * j:8 * j + 8, :] = v
        for j in range((rows - CELLS) // 8):
            v = tails[0][8 * j:8 * j + 8]
            for r in range(1, rows_owned):
                v = jnp.where(hits_r[r], tails[r][8 * j:8 * j + 8], v)
            pay_ref[d, CELLS + 8 * j:CELLS + 8 * j + 8, :] = v
        return carry

    lax.fori_loop(0, sources, scatter, 0, unroll=4)


def final_kernel(
    recv_ref, prior_ref, sums_ref, w_ref, maps_ref, feed_ref,
    x_ref, r_ref, out_ref,
    gram_ref, y0_ref, y1_ref,
    *, slots, feeds, samples,
):
    sources, rows, lanes = recv_ref.shape
    width = lanes // 2
    nb = lanes // CELLS
    rb = CELLS // nb
    share = rb // feeds
    prior = prior_ref[...]
    mean = shift_of(prior)
    offset = prior - mean
    sigma = mean + float(samples)
    scal = jnp.sum(recv_ref[:, CELLS + share:CELLS + share + 2, :], axis=0)
    rr0 = jnp.sum(scal[0:1, 0:width], axis=1, keepdims=True)
    rz = jnp.sum(scal[0:1, width:lanes], axis=1, keepdims=True)
    zz = jnp.sum(scal[1:2, 0:width], axis=1, keepdims=True)
    zw = jnp.sum(scal[1:2, width:lanes], axis=1, keepdims=True)
    gamma = rz / rr0
    alpha0 = 1.0 / (sigma + gamma)
    ee = zz - gamma * rz
    rr1 = alpha0 * alpha0 * ee
    beta = rr1 / rr0
    e_a_e = sigma * ee + (zw - 2.0 * gamma * zz + gamma * gamma * rz)
    alpha1 = rr1 / (alpha0 * alpha0 * e_a_e - rr1 * beta / alpha0)
    lead = alpha0 * gamma + beta
    slack = 1.0 - alpha1 * sigma
    x_r = alpha0 + alpha1 * lead
    x_z = -alpha0 * alpha1
    r_r = alpha0 * gamma * slack - alpha1 * sigma * beta
    r_z = -alpha0 * slack - alpha1 * lead
    r_w = alpha0 * alpha1
    gram_ref[...] = jnp.zeros(gram_ref.shape, f32)
    for k in range(slots):
        pack = jnp.concatenate(
            [recv_ref[f * slots + k, CELLS:CELLS + share, :] for f in range(feeds)], axis=0
        )
        expand(gram_ref, k, pack, nb, rb)
        y0_ref[k * CELLS:(k + 1) * CELLS, :] = jnp.concatenate(
            [recv_ref[f * slots + k, 0:CELLS, 0:width] for f in range(feeds)], axis=1
        )
        y1_ref[k * CELLS:(k + 1) * CELLS, :] = jnp.concatenate(
            [recv_ref[f * slots + k, 0:CELLS, width:lanes] for f in range(feeds)], axis=1
        )
    gram = gram_ref[...]
    hits = jnp.sum(gram, axis=1, keepdims=True) / float(samples)
    inverse = 1.0 / jnp.maximum(hits, 1.0)
    y0 = y0_ref[...]
    y1 = y1_ref[...]
    y2 = offset * y1 - inverse * jnp.dot(gram, y1, precision=EXACT, preferred_element_type=f32)
    sums = sums_ref[...]
    w = w_ref[...]
    lead_x = x_r + x_z * offset
    x_ref[...] = lead_x * sums - counted(w, lead_x * y0 + x_z * y1)
    second = r_z + r_w * offset
    lead_r = r_r + second * offset
    r_ref[...] = lead_r * sums - counted(w, lead_r * y0 + second * y1 + r_w * y2)
    out_ref[...] = maps_ref[0] - x_r * maps_ref[1] - x_z * maps_ref[2]


def local(tod, pixels, block_slots, tile_lists, tile_place, prior):
    axes = ("feed", "tm")
    feeds = lax.axis_size("feed")
    owners = lax.axis_size("tm")
    slots = tile_lists.shape[1] * tile_lists.shape[2]
    assert slots == owners
    rows_owned = tile_place.shape[0] // owners
    blocks, samples, channels = tod.shape
    cells = slots * CELLS
    width = channels // feeds
    lanes = 2 * width
    gram_rows = CELLS * CELLS // lanes
    rows = CELLS + gram_rows
    devices = feeds * owners
    step_samples = max(n for n in range(1, 11) if samples % n == 0)
    smem = pl.BlockSpec(memory_space=pltpu.SMEM)
    vmem = pl.BlockSpec(memory_space=pltpu.VMEM)

    def whole(*shape):
        return pl.BlockSpec(shape, lambda i: (0,) * len(shape))

    payload, sums, weights, power = pl.pallas_call(
        lambda *refs: bin_kernel(
            *refs, slots=slots, feeds=feeds, rows_owned=rows_owned, step_samples=step_samples
        ),
        grid=(samples // step_samples,),
        in_specs=[
            smem,
            smem,
            whole(1, blocks),
            whole(samples, blocks),
            pl.BlockSpec((step_samples, blocks, channels), lambda i: (i, 0, 0)),
        ],
        out_specs=[
            whole(devices, rows, lanes),
            whole(blocks, channels),
            whole(blocks, cells),
            whole(1, channels),
        ],
        out_shape=[
            jax.ShapeDtypeStruct((devices, rows, lanes), f32),
            jax.ShapeDtypeStruct((blocks, channels), f32),
            jax.ShapeDtypeStruct((blocks, cells), bf16),
            jax.ShapeDtypeStruct((1, channels), f32),
        ],
        scratch_shapes=[
            pltpu.VMEM((cells, channels), f32),
            pltpu.VMEM((blocks, channels), f32),
            pltpu.VMEM((cells, blocks), f32),
            pltpu.VMEM((cells, cells), f32),
            pltpu.VMEM((cells, channels), f32),
        ],
        name="bin_samples",
    )(
        tile_lists.reshape(slots),
        tile_place,
        block_slots.reshape(1, blocks),
        pixels.T,
        tod.transpose(1, 0, 2),
    )
    received = lax.all_to_all(payload, axes, split_axis=0, concat_axis=0, tiled=True)
    feed = lax.axis_index("feed").astype(jnp.int32).reshape(1)
    prior_row = prior.reshape(1, channels)
    owned_cells = rows_owned * CELLS
    answer, maps = pl.pallas_call(
        lambda *refs: owner_kernel(*refs, feeds=feeds, rows_owned=rows_owned, samples=samples),
        in_specs=[smem, vmem, vmem, vmem],
        out_specs=[vmem, vmem],
        out_shape=[
            jax.ShapeDtypeStruct((devices, rows, lanes), f32),
            jax.ShapeDtypeStruct((3, owned_cells, width), f32),
        ],
        scratch_shapes=[
            pltpu.VMEM((rows_owned, rows, lanes), f32),
            pltpu.VMEM((owned_cells, owned_cells), f32),
            pltpu.VMEM((owned_cells, lanes), f32),
        ],
        name="solve_tiles",
    )(feed, received, prior_row, power)
    returned = lax.all_to_all(answer, axes, split_axis=0, concat_axis=0, tiled=True)
    drift, leftover, sky = pl.pallas_call(
        lambda *refs: final_kernel(*refs, slots=slots, feeds=feeds, samples=samples),
        in_specs=[vmem, vmem, vmem, vmem, vmem, smem],
        out_specs=[vmem, vmem, vmem],
        out_shape=[
            jax.ShapeDtypeStruct((blocks, channels), f32),
            jax.ShapeDtypeStruct((blocks, channels), f32),
            jax.ShapeDtypeStruct((owned_cells, width), f32),
        ],
        scratch_shapes=[
            pltpu.VMEM((cells, cells), f32),
            pltpu.VMEM((cells, channels), f32),
            pltpu.VMEM((cells, channels), f32),
        ],
        name="finish",
    )(returned, prior_row, sums, weights, maps, feed)
    return drift, leftover, sky.reshape(rows_owned, CELLS, width)


def solution(mesh):
    return jax.shard_map(
        local,
        mesh=mesh,
        in_specs=(
            P(("feed", "tm"), None, None),
            P(("feed", "tm"), None),
            P(("feed", "tm")),
            P(("feed", "tm"), None, None),
            P(),
            P(),
        ),
        out_specs=(P(("feed", "tm"), None), P(("feed", "tm"), None), P("tm", None, "feed")),
        check_vma=False,
    )
```

time: 405 us -> 68.2 us (0.17)
  blocking collectives: 201 us -> 22.4 us
  waiting for transfers between devices: 131 us -> 19 us
  matrix products: 28.3 us -> 0 us
  Pallas kernels: 0 us -> 17.6 us
  between operations: 18 us -> 0.65 us
  starting transfers between devices: 16.9 us -> 7.32 us
  other arithmetic: 4.82 us -> 0 us
    psum x4 -> x0, waiting for transfers between devices: 124 us -> none  [averaged_patch_lines(): summed = lax.psum(owned_sum, 'feed')]
    psum x4 -> x0, blocking collectives: 123 us -> none  [the longest x2 79.4 us: squares(): return lax.psum(jnp.sum(values * values), ('feed', 'tm'))]
    all_to_all x6 -> x1, blocking collectives: 77.4 us -> 22.4 us  [local(): lax.all_to_all(answer, axes, split_axis=0, concat_axis=0, tiled=True)]
    dot_general x16 -> x0, matrix products: 28.3 us -> none  [the longest x1 7.73 us: local(): jnp.einsum('bsp,bsc->bpc', pix_hot, tod, preferred_element_type=jnp.float32)]
    pallas_call x0 -> x3, Pallas kernels: none -> 17.6 us  [the longest x1 8.49 us: local(): pl.pallas_call(lambda *refs: bin_kernel(*refs, slots=slots, feeds=feeds,...]
    all_to_all x3 -> x1, waiting for transfers between devices: 7.18 us -> 19 us  [local(): lax.all_to_all(payload, axes, split_axis=0, concat_axis=0, tiled=True)]
    all_to_all x3 -> x1, starting transfers between devices: 16.7 us -> 7.32 us  [local(): lax.all_to_all(payload, axes, split_axis=0, concat_axis=0, tiled=True)]
  transfers between devices with their start and end apart: 7 -> 1, of which waited for: 6 -> 1; matrix products, arithmetic and copies ran while one was open for 5% -> 0% of each run, Pallas kernels for 0% -> 0%
where the time goes in v1:
time: 68.2 us; the launch traced here: 67.8 us
  blocking collectives  22.4 us (33%)
  waiting for transfers between devices  19 us (28%)
  Pallas kernels  17.6 us (26%)
  starting transfers between devices  7.32 us (11%)
  local copies, waits for them, and re-layouts  0.84 us (1%)
    all_to_all x1, blocking collectives, local(): lax.all_to_all(answer, axes, split_axis=0, concat_axis=0, tiled=True)  22.4 us
    all_to_all x1, waiting for transfers between devices, local(): lax.all_to_all(payload, axes, split_axis=0, concat_axis=0, tiled=True)  19 us
    pallas_call x1, Pallas kernels, local(): pl.pallas_call(lambda *refs: bin_kernel(*refs, slots=slots, feeds=feeds,...  8.49 us
    all_to_all x1, starting transfers between devices, local(): lax.all_to_all(payload, axes, split_axis=0, concat_axis=0, tiled=True)  7.32 us
    pallas_call x1, Pallas kernels, local(): pl.pallas_call(lambda *refs: owner_kernel(*refs, feeds=feeds, rows_owned=...  5.95 us
    pallas_call x1, Pallas kernels, local(): pl.pallas_call(lambda *refs: final_kernel(*refs, slots=slots, feeds=feeds...  3.17 us
  transfers between devices with their start and end apart: 1, of which 1 were waited for; matrix products, arithmetic and copies ran while one was open for 0% of the time, Pallas kernels for 0%

profile of v1, /device:TPU:0, one launch (start us, length us, event | category | flops | bytes accessed | tf_op | source)
XLA Modules:
  0.0 67.8 jit_solution(15111356565450933210)
XLA Ops:
  0.6 8.5 %bin_samples.1 = (f32[32,40,128]{2,1,0:T(8,128)}, f32[256,256]{1,0:T(8,128)}, bf16[256,256]{1,0:T(8,128)(2,1)}, f32[1,256]{1,0:T(1,128)}) custom-call(s32[8]{0:T(128)} %bitcast.12, s32[64]{0:T(128)} %refs_1_.1, s32[1,256]{1,0:T(1,128)} %bitcast.11, s32[50,256]{1,0:T(8,128)} %bitcast.8, bf16[50,256,256]{2,1,0:T(8,128)(2,1)} %bitcast.7), custom_call_target="tpu_custom_call" | custom-call | tf_op jit(solution)/shard_map/bin_samples/pallas_call | solution.py:298
  9.1 7.3 %all-to-all-start = ((f32[32,40,128]{2,1,0:T(8,128)}), f32[32,40,128]{2,1,0:T(8,128)S(1)}, u32[]{:S(2)}, u32[]{:S(2)}) async-start(f32[32,40,128]{2,1,0:T(8,128)} %get-tuple-element.12), calls=%async_computation | async-start | bytes 1310720 | tf_op jit(solution)/shard_map/all_to_all | solution.py:337
  16.5 19.0 %all-to-all-done.refs_1_ = f32[32,40,128]{2,1,0:T(8,128)S(1)} async-done(((f32[32,40,128]{2,1,0:T(8,128)}), f32[32,40,128]{2,1,0:T(8,128)S(1)}, u32[]{:S(2)}, u32[]{:S(2)}) %all-to-all-start) | async-done | bytes 655392 | tf_op jit(solution)/shard_map/all_to_all | solution.py:337
  35.5 0.0 copy-start
  35.5 0.8 %copy-done = f32[32,40,128]{2,1,0:T(8,128)} copy-done((f32[32,40,128]{2,1,0:T(8,128)}, f32[32,40,128]{2,1,0:T(8,128)S(1)}, u32[]{:S(2)}) %copy-start) | copy-done | bytes 655384
  36.3 5.9 %solve_tiles.1 = (f32[32,40,128]{2,1,0:T(8,128)}, f32[3,256,64]{2,1,0:T(8,128)}) custom-call(s32[1]{0:T(128)} %bitcast.refs_0_.refs_5_, f32[32,40,128]{2,1,0:T(8,128)} %copy-done, f32[1,256]{1,0:T(1,128)} %bitcast.9, f32[1,256]{1,0:T(1,128)} %get-tuple-element.13.refs_3_), custom_call_target="tpu_custom_call" | custom-call | tf_op jit(solution)/shard_map/solve_tiles/pallas_call | solution.py:341
  42.3 22.4 %all_to_all.10.refs_0_ = f32[32,40,128]{2,1,0:T(8,128)} all-to-all(f32[32,40,128]{2,1,0:T(8,128)} %get-tuple-element.14), channel_id=1, replica_groups=mesh['feed'=4,'tm'=8] {'feed','tm'}, dimensions={0} | all-to-all | bytes 1310720 | tf_op jit(solution)/shard_map/all_to_all | solution.py:356
  64.6 3.2 %finish.1 = (f32[256,256]{1,0:T(8,128)}, f32[256,256]{1,0:T(8,128)}, f32[256,64]{1,0:T(8,128)}) custom-call(f32[32,40,128]{2,1,0:T(8,128)} %all_to_all.10.refs_0_, f32[1,256]{1,0:T(1,128)} %bitcast.10, f32[256,256]{1,0:T(8,128)} %get-tuple-element.15.refs_2_, bf16[256,256]{1,0:T(8,128)(2,1)} %get-tuple-element.16.refs_3_, ...), custom_call_target="tpu_custom_call" | custom-call | tf_op jit(solution)/shard_map/finish/pallas_call | solution.py:357
Async XLA Ops:
  9.1 26.4 %all-to-all-start = ((f32[32,40,128]{2,1,0:T(8,128)}), f32[32,40,128]{2,1,0:T(8,128)S(1)}, u32[]{:S(2)}, u32[]{:S(2)}) async-start(f32[32,40,128]{2,1,0:T(8,128)} %get-tuple-element.12), calls=%async_computation | async-start | bytes 1310720 | tf_op jit(solution)/shard_map/all_to_all | solution.py:337
  35.5 0.8 %copy-start = (f32[32,40,128]{2,1,0:T(8,128)}, f32[32,40,128]{2,1,0:T(8,128)S(1)}, u32[]{:S(2)}) copy-start(f32[32,40,128]{2,1,0:T(8,128)S(1)} %all-to-all-done.refs_1_) | copy-start | bytes 1966084

commit v2 on v1

v2 whole, which is shorter than its diff:
```python
import jax
import jax.numpy as jnp
from jax import lax
from jax.experimental import pallas as pl
from jax.experimental.pallas import tpu as pltpu
from jax.sharding import PartitionSpec as P

CELLS = 32
EXACT = lax.Precision.HIGHEST
f32 = jnp.float32
bf16 = jnp.bfloat16


def split3(value):
    high = value.astype(bf16)
    rest = value - high.astype(f32)
    mid = rest.astype(bf16)
    low = (rest - mid.astype(f32)).astype(bf16)
    return high, mid, low


def counted(counts, value):
    out = None
    for part in split3(value):
        term = jnp.dot(counts, part, preferred_element_type=f32)
        out = term if out is None else out + term
    return out


def near(value, small):
    return pltpu.with_memory_space_constraint(value, pltpu.VMEM) if small else value


def shift_of(prior):
    return jnp.sum(prior, axis=1, keepdims=True) * (1.0 / prior.shape[1])


def bin_kernel(
    feed_ref, list_ref, place_ref, slot_ref, pix_ref, tod_ref,
    pay_ref, sums_ref, w_ref, power_ref,
    tod_buf, hot_ref, t_acc, wt_acc, sems,
    *, slots, feeds, rows_owned, chunk,
):
    samples, blocks, channels = tod_ref.shape
    cells = slots * CELLS
    lanes = pay_ref.shape[2]
    width = lanes // 2
    chunks = samples // chunk
    kind = bf16 if cells <= 256 else f32
    copies = [
        pltpu.make_async_copy(
            tod_ref.at[pl.ds(i * chunk, chunk)], tod_buf.at[pl.ds(i * chunk, chunk)], sems.at[i]
        )
        for i in range(chunks)
    ]
    for copy in copies:
        copy.start()
    base = slot_ref[...] * CELLS
    one = jnp.ones((), kind)
    nil = jnp.zeros((), kind)

    def mark_hot(i):
        spread = [
            jnp.broadcast_to((base + pix_ref[s:s + 1, :]).astype(f32).astype(kind), (16, blocks))
            for s in range(i * chunk, (i + 1) * chunk)
        ]
        for q in range(0, cells, 16):
            row = (lax.broadcasted_iota(jnp.int32, (16, blocks), 0) + q).astype(f32).astype(kind)
            count = None
            for j in range(chunk):
                s = i * chunk + j
                hot = jnp.where(row == spread[j], one, nil)
                hot_ref[q:q + 16, s * blocks:(s + 1) * blocks] = hot.astype(bf16)
                count = hot if count is None else count + hot
            if i > 0:
                count = count + wt_acc[q:q + 16, :]
            wt_acc[q:q + 16, :] = count

    def pack_counts():
        wt = wt_acc[...].astype(bf16)
        w_ref[...] = wt.T
        nb = lanes // CELLS
        rb = CELLS // nb
        every = wt_acc[0:CELLS, :].astype(f32)
        for k in range(1, slots):
            every = every + wt_acc[k * CELLS:(k + 1) * CELLS, :].astype(f32)
        every = jnp.concatenate([every.astype(bf16)] * nb, axis=0)
        gram = lax.dot_general(wt, every, (((1,), (1,)), ((), ())), preferred_element_type=f32)
        sub = lax.broadcasted_iota(jnp.int32, (rb, lanes), 0)
        lane = lax.broadcasted_iota(jnp.int32, (rb, lanes), 1)
        mark = (sub == rb - 1) & (lane == (nb - 1) * CELLS)
        for k in range(slots):
            pack = gram[k * CELLS:k * CELLS + rb]
            for i in range(1, nb):
                piece = gram[k * CELLS + rb * i:k * CELLS + rb * (i + 1)]
                pack = jnp.where(lane >= i * CELLS, piece, pack)
            tile = list_ref[k]
            row = jnp.where(tile >= 0, lax.rem(place_ref[jnp.maximum(tile, 0)], rows_owned), -1)
            pack = jnp.where(mark, row.astype(f32), pack)
            for f in range(feeds):
                pay_ref[f * slots + k, CELLS:CELLS + rb, :] = pack

    mark_hot(0)
    for i in range(chunks):
        if i + 1 < chunks:
            mark_hot(i + 1)
        else:
            pack_counts()
        copies[i].wait()
        first = i * chunk
        now = tod_buf[first:first + chunk].reshape(chunk * blocks, channels)
        binned = jnp.dot(
            hot_ref[:, first * blocks:(first + chunk) * blocks], now, preferred_element_type=f32
        )
        t_acc[...] = binned if i == 0 else t_acc[...] + binned
        for b in range(0, blocks, 16):
            total = sums_ref[b:b + 16, :] if i else None
            for s in range(first, first + chunk):
                part = tod_buf[s, b:b + 16, :].astype(f32)
                total = part if total is None else total + part
            sums_ref[b:b + 16, :] = total

    sums = sums_ref[...]
    power_ref[...] = jnp.sum(sums * sums, axis=0, keepdims=True)
    cross = counted(wt_acc[...].astype(bf16), sums)
    for k in range(slots):
        q0 = k * CELLS
        for f in range(feeds):
            pay_ref[f * slots + k, 0:CELLS, :] = jnp.concatenate(
                [
                    t_acc[q0:q0 + CELLS, f * width:(f + 1) * width],
                    cross[q0:q0 + CELLS, f * width:(f + 1) * width],
                ],
                axis=1,
            )


def turn(value, shift):
    lanes = value.shape[1]
    shift = shift % lanes
    if shift == 0:
        return value
    if lanes % 128 == 0:
        return pltpu.roll(value, shift, 1)
    return jnp.concatenate([value[:, lanes - shift:], value[:, :lanes - shift]], axis=1)


def gram_blocks(packs):
    rb, lanes = packs[0].shape
    nb = lanes // CELLS
    lane = lax.broadcasted_iota(jnp.int32, (rb, lanes), 1)
    blocks = []
    for first in range(0, len(packs), nb):
        rows = []
        for j in range(nb):
            inside = (lane >= j * CELLS) & (lane < (j + 1) * CELLS)
            for i in range(nb):
                rows.append(jnp.where(inside, turn(packs[first + j], (j - i) * CELLS), 0.0))
        blocks.append(jnp.concatenate(rows, axis=0))
    return blocks


def stacked(block):
    return jnp.concatenate(split3(block), axis=0)


def gram_times(stack, value):
    n = stack.shape[1]
    total = None
    for j, part in enumerate(split3(value)):
        term = jnp.dot(stack[0:(3 - j) * n], part, preferred_element_type=f32)
        for i in range(3 - j):
            piece = term[i * n:(i + 1) * n]
            total = piece if total is None else total + piece
    return total


def gram_times_narrow(stack, value):
    n = stack.shape[1]
    w = value.shape[1]
    wide = jnp.dot(stack, jnp.concatenate(split3(value), axis=1), preferred_element_type=f32)
    wide = wide[2 * n:3 * n] + wide[n:2 * n] + wide[0:n]
    return wide[:, 2 * w:3 * w] + wide[:, w:2 * w] + wide[:, 0:w]


def owner_kernel(
    feed_ref, recv_ref, prior_ref, power_ref,
    pay_ref, map_ref,
    index_ref, acc_ref, pair_ref,
    *, feeds, rows_owned, samples, rows_out,
):
    sources, rows, lanes = recv_ref.shape
    width = lanes // 2
    nb = lanes // CELLS
    rb = CELLS // nb
    share = rb // feeds
    tiles = rows // 8
    mark_row = CELLS + rb - 1
    mark_lane = (nb - 1) * CELLS
    step = 8

    def spread(g, carry):
        for e in range(step):
            d = g * step + e
            index_ref[d] = jnp.broadcast_to(
                recv_ref[d, mark_row:mark_row + 1, mark_lane:mark_lane + 1], (8, lanes)
            )
        return carry

    lax.fori_loop(0, sources // step, spread, 0)
    for group in range(0, tiles, 2):
        members = range(group, min(group + 2, tiles))

        def gather(g, accs):
            accs = list(accs)
            for e in range(step):
                d = g * step + e
                index = index_ref[d]
                values = [recv_ref[d, 8 * j:8 * j + 8, :] for j in members]
                for r in range(rows_owned):
                    hit = index == float(r)
                    for n, value in enumerate(values):
                        at = r * len(values) + n
                        accs[at] = accs[at] + jnp.where(hit, value, 0.0)
            return tuple(accs)

        zero = jnp.zeros((8, lanes), f32)
        accs = lax.fori_loop(0, sources // step, gather, (zero,) * (rows_owned * len(members)))
        for r in range(rows_owned):
            for n, j in enumerate(members):
                acc_ref[r, 8 * j:8 * j + 8, :] = accs[r * len(members) + n]

    sub = lax.broadcasted_iota(jnp.int32, (rb, lanes), 0)
    lane = lax.broadcasted_iota(jnp.int32, (rb, lanes), 1)
    mark = (sub == rb - 1) & (lane == mark_lane)
    packs = []
    for r in range(rows_owned):
        pack = acc_ref[r, CELLS:CELLS + rb, :]
        packs.append(jnp.where(mark, pack[0:1, CELLS - 1:CELLS], pack))
    prior = prior_ref[...]
    offset = prior - shift_of(prior)
    feed = feed_ref[0]
    mine = offset[:, 0:width]
    for f in range(1, feeds):
        mine = jnp.where(feed == f, offset[:, f * width:(f + 1) * width], mine)
    rr = rz = zz = zw = None
    cross = half = last = None
    for g, block in enumerate(gram_blocks(packs)):
        stack = stacked(block)
        hits = jnp.sum(block, axis=1, keepdims=True) / float(samples)
        inverse = 1.0 / jnp.maximum(hits, 1.0)
        both = jnp.concatenate([acc_ref[r, 0:CELLS, :] for r in range(g * nb, (g + 1) * nb)], axis=0)
        v_sum = both[:, width:lanes]
        y0 = both[:, 0:width] * inverse
        u0 = v_sum - gram_times_narrow(stack, y0)
        y1 = u0 * inverse
        uz = mine * u0 - gram_times_narrow(stack, y1)
        y2 = uz * inverse
        q0 = g * nb * CELLS
        map_ref[0, q0:q0 + nb * CELLS, :] = y0
        map_ref[1, q0:q0 + nb * CELLS, :] = y1
        map_ref[2, q0:q0 + nb * CELLS, :] = y2
        pair_ref[q0:q0 + nb * CELLS, :] = jnp.concatenate([y0, y1], axis=1)
        terms = [
            jnp.sum(term, axis=0, keepdims=True)
            for term in (y0 * (v_sum + u0), u0 * y1, y1 * (mine * u0 + uz), uz * y2)
        ]
        if g == 0:
            rr, cross, half, last = terms
        else:
            rr, cross, half, last = rr + terms[0], cross + terms[1], half + terms[2], last + terms[3]
    rr = -rr
    rz = mine * rr - cross
    zz = mine * mine * rr - half
    zw = mine * zz - last
    power = power_ref[...]
    parts = []
    for own in (rr, rz, zz, zw):
        for f in range(feeds):
            own = own + power[:, f * width:(f + 1) * width]
        parts.append(own[:, 0:width // 2] + own[:, width // 2:width])
        power = power * offset
    scal = jnp.concatenate(parts, axis=1)
    tails = []
    for r in range(rows_owned):
        quarter = packs[r][0:share]
        for f in range(1, feeds):
            quarter = jnp.where(feed == f, packs[r][f * share:(f + 1) * share], quarter)
        tails.append(quarter)

    def scatter(d):
        index = index_ref[d]
        hits_r = [index == float(r) for r in range(rows_owned)]
        for j in range(CELLS // 8):
            v = pair_ref[8 * j:8 * j + 8, :]
            for r in range(1, rows_owned):
                v = jnp.where(hits_r[r], pair_ref[r * CELLS + 8 * j:r * CELLS + 8 * j + 8, :], v)
            pay_ref[pl.ds(d * rows_out + 8 * j, 8), :] = v
        v = tails[0]
        for r in range(1, rows_owned):
            v = jnp.where(hits_r[r][0:share], tails[r], v)
        if rows_out % 8:
            pay_ref[pl.ds(d * rows_out + CELLS, share + 1), :] = jnp.concatenate([v, scal], axis=0)
        else:
            fill = jnp.zeros((rows_out - CELLS - share - 1, lanes), f32)
            pay_ref[pl.ds(d * rows_out + CELLS, 8), :] = jnp.concatenate([v, scal, fill], axis=0)

    if rows_out % 8:
        for d in range(sources):
            scatter(d)
    else:
        lax.fori_loop(0, sources, lambda d, c: (scatter(d), c)[1], 0)


def final_kernel(
    recv_ref, prior_ref, sums_ref, w_ref, maps_ref,
    x_ref, r_ref, out_ref,
    y0_ref, y1_ref, y2_ref,
    *, slots, feeds, samples, share, rows_in,
):
    lanes = recv_ref.shape[1]
    sources = recv_ref.shape[0] // rows_in
    width = lanes // 2
    nb = lanes // CELLS
    prior = prior_ref[...]
    mean = shift_of(prior)
    offset = prior - mean
    sigma = mean + float(samples)
    scal = None
    for d in range(sources):
        now = recv_ref[d * rows_in + CELLS + share:d * rows_in + CELLS + share + 1, :]
        scal = now if scal is None else scal + now
    quarter = lanes // 4
    rr0, rz, zz, zw = [
        jnp.sum(scal[:, i * quarter:(i + 1) * quarter], axis=1, keepdims=True) for i in range(4)
    ]
    gamma = rz / rr0
    alpha0 = 1.0 / (sigma + gamma)
    ee = zz - gamma * rz
    rr1 = alpha0 * alpha0 * ee
    beta = rr1 / rr0
    e_a_e = sigma * ee + (zw - 2.0 * gamma * zz + gamma * gamma * rz)
    alpha1 = rr1 / (alpha0 * alpha0 * e_a_e - rr1 * beta / alpha0)
    lead = alpha0 * gamma + beta
    slack = 1.0 - alpha1 * sigma
    x_r = alpha0 + alpha1 * lead
    x_z = -alpha0 * alpha1
    r_r = alpha0 * gamma * slack - alpha1 * sigma * beta
    r_z = -alpha0 * slack - alpha1 * lead
    r_w = alpha0 * alpha1
    packs = []
    for k in range(slots):
        base = [(f * slots + k) * rows_in for f in range(feeds)]
        packs.append(
            jnp.concatenate([recv_ref[b + CELLS:b + CELLS + share, :] for b in base], axis=0)
        )
        y0_ref[k * CELLS:(k + 1) * CELLS, :] = jnp.concatenate(
            [recv_ref[b:b + CELLS, 0:width] for b in base], axis=1
        )
        y1_ref[k * CELLS:(k + 1) * CELLS, :] = jnp.concatenate(
            [recv_ref[b:b + CELLS, width:lanes] for b in base], axis=1
        )
    for g, block in enumerate(gram_blocks(packs)):
        stack = stacked(block)
        hits = jnp.sum(block, axis=1, keepdims=True) / float(samples)
        inverse = 1.0 / jnp.maximum(hits, 1.0)
        q0 = g * nb * CELLS
        y1 = y1_ref[q0:q0 + nb * CELLS, :]
        y2_ref[q0:q0 + nb * CELLS, :] = offset * y1 - inverse * gram_times(stack, y1)
    y0 = y0_ref[...]
    y1 = y1_ref[...]
    sums = sums_ref[...]
    w = w_ref[...]
    lead_x = x_r + x_z * offset
    x_ref[...] = lead_x * sums - counted(w, lead_x * y0 + x_z * y1)
    second = r_z + r_w * offset
    lead_r = r_r + second * offset
    r_ref[...] = lead_r * sums - counted(w, lead_r * y0 + second * y1 + r_w * y2_ref[...])
    out_ref[...] = maps_ref[0] - x_r * maps_ref[1] - x_z * maps_ref[2]


def local(tod, pixels, block_slots, tile_lists, tile_place, prior):
    axes = ("feed", "tm")
    feeds = lax.axis_size("feed")
    owners = lax.axis_size("tm")
    slots = tile_lists.shape[1] * tile_lists.shape[2]
    assert slots == owners
    rows_owned = tile_place.shape[0] // owners
    blocks, samples, channels = tod.shape
    cells = slots * CELLS
    width = channels // feeds
    lanes = 2 * width
    gram_rows = CELLS * CELLS // lanes
    rows = CELLS + gram_rows
    devices = feeds * owners
    chunk = max(n for n in range(1, 11) if samples % n == 0)
    small = devices * rows * lanes <= 1 << 18
    held = pltpu.VMEM if small else jax.ShapeDtypeStruct
    smem = pl.BlockSpec(memory_space=pltpu.SMEM)
    vmem = pl.BlockSpec(memory_space=pltpu.VMEM)

    feed = lax.axis_index("feed").astype(jnp.int32).reshape(1)
    payload, sums, weights, power = pl.pallas_call(
        lambda *refs: bin_kernel(*refs, slots=slots, feeds=feeds, rows_owned=rows_owned, chunk=chunk),
        in_specs=[smem, smem, smem, vmem, vmem, pl.BlockSpec(memory_space=pl.ANY)],
        out_specs=[vmem, vmem, vmem, vmem],
        out_shape=[
            held((devices, rows, lanes), f32),
            held((blocks, channels), f32),
            held((blocks, cells), bf16),
            held((1, channels), f32),
        ],
        scratch_shapes=[
            pltpu.VMEM((samples, blocks, channels), bf16),
            pltpu.VMEM((cells, samples * blocks), bf16),
            pltpu.VMEM((cells, channels), f32),
            pltpu.VMEM((cells, blocks), bf16 if cells <= 256 else f32),
            pltpu.SemaphoreType.DMA((samples // chunk,)),
        ],
        name="bin_samples",
    )(
        feed,
        tile_lists.reshape(slots),
        tile_place,
        block_slots.reshape(1, blocks),
        pixels.T,
        tod.transpose(1, 0, 2),
    )
    received = lax.all_to_all(payload, axes, split_axis=0, concat_axis=0, tiled=True)
    prior_row = prior.reshape(1, channels)
    owned_cells = rows_owned * CELLS
    share = gram_rows // feeds
    rows_back = CELLS + share + 1
    if not small:
        rows_back = -(-rows_back // 8) * 8
    answer, maps = pl.pallas_call(
        lambda *refs: owner_kernel(
            *refs, feeds=feeds, rows_owned=rows_owned, samples=samples, rows_out=rows_back
        ),
        in_specs=[smem, vmem, vmem, vmem],
        out_specs=[vmem, vmem],
        out_shape=[
            held((devices * rows_back, lanes), f32),
            held((3, owned_cells, width), f32),
        ],
        scratch_shapes=[
            pltpu.VMEM((devices, 8, lanes), f32),
            pltpu.VMEM((rows_owned, rows, lanes), f32),
            pltpu.VMEM((owned_cells, lanes), f32),
        ],
        name="solve_tiles",
    )(feed, near(received, small), prior_row, near(power, small))
    returned = lax.all_to_all(
        answer.reshape(devices, 1, rows_back * lanes), axes, split_axis=0, concat_axis=0, tiled=True
    ).reshape(devices * rows_back, lanes)
    drift, leftover, sky = pl.pallas_call(
        lambda *refs: final_kernel(
            *refs, slots=slots, feeds=feeds, samples=samples, share=share, rows_in=rows_back
        ),
        in_specs=[vmem, vmem, vmem, vmem, vmem],
        out_specs=[vmem, vmem, vmem],
        out_shape=[
            jax.ShapeDtypeStruct((blocks, channels), f32),
            jax.ShapeDtypeStruct((blocks, channels), f32),
            jax.ShapeDtypeStruct((owned_cells, width), f32),
        ],
        scratch_shapes=[
            pltpu.VMEM((cells, channels), f32),
            pltpu.VMEM((cells, channels), f32),
            pltpu.VMEM((cells, channels), f32),
        ],
        name="finish",
    )(near(returned, small), prior_row, near(sums, small), near(weights, small), near(maps, small))
    return drift, leftover, sky.reshape(rows_owned, CELLS, width)


def solution(mesh):
    return jax.shard_map(
        local,
        mesh=mesh,
        in_specs=(
            P(("feed", "tm"), None, None),
            P(("feed", "tm"), None),
            P(("feed", "tm")),
            P(("feed", "tm"), None, None),
            P(),
            P(),
        ),
        out_specs=(P(("feed", "tm"), None), P(("feed", "tm"), None), P("tm", None, "feed")),
        check_vma=False,
    )
```

time: 68.2 us -> 58.7 us (0.86)
  blocking collectives: 22.4 us -> 45.6 us
  waiting for transfers between devices: 19 us -> 0 us
  starting transfers between devices: 7.32 us -> 0 us
  Pallas kernels: 17.6 us -> 12.2 us
  local copies, waits for them, and re-layouts: 0.84 us -> 0 us
    all_to_all x1 -> x2, blocking collectives: 22.4 us -> 45.6 us  [the longest x1 26.2 us: local(): lax.all_to_all(payload, axes, split_axis=0, concat_axis=0, tiled=True)]
    all_to_all x1 -> x0, waiting for transfers between devices: 19 us -> none  [local(): lax.all_to_all(payload, axes, split_axis=0, concat_axis=0, tiled=True)]
    all_to_all x1 -> x0, starting transfers between devices: 7.32 us -> none  [local(): lax.all_to_all(payload, axes, split_axis=0, concat_axis=0, tiled=True)]
    pallas_call x1, Pallas kernels: 5.95 us -> 3.51 us  [local(): pl.pallas_call(lambda *refs: owner_kernel(*refs, feeds=feeds, rows_owned=...]
    pallas_call x1, Pallas kernels: 8.49 us -> 6.19 us  [local(): pl.pallas_call(lambda *refs: bin_kernel(*refs, slots=slots, feeds=feeds,...]
    unnamed x2 -> x0, local copies, waits for them, and re-layouts: 0.84 us -> none
    pallas_call x1, Pallas kernels: 3.17 us -> 2.48 us  [local(): pl.pallas_call(lambda *refs: final_kernel(*refs, slots=slots, feeds=feeds...]
  transfers between devices with their start and end apart: 1 -> 0, of which waited for: 1 -> 0; matrix products, arithmetic and copies ran while one was open for 0% -> 0% of each run, Pallas kernels for 0% -> 0%
where the time goes in v2:
time: 58.7 us; the launch traced here: 58.5 us
  blocking collectives  45.6 us (78%)
  Pallas kernels  12.2 us (21%)
  between operations  0.65 us (1%)
    all_to_all x1, blocking collectives, local(): lax.all_to_all(payload, axes, split_axis=0, concat_axis=0, tiled=True)  26.2 us
    all_to_all x1, blocking collectives, local(): lax.all_to_all(answer.reshape(devices, 1, rows_back * lanes), axes, split...  19.4 us
    pallas_call x1, Pallas kernels, local(): pl.pallas_call(lambda *refs: bin_kernel(*refs, slots=slots, feeds=feeds,...  6.19 us
    pallas_call x1, Pallas kernels, local(): pl.pallas_call(lambda *refs: owner_kernel(*refs, feeds=feeds, rows_owned=...  3.51 us
    pallas_call x1, Pallas kernels, local(): pl.pallas_call(lambda *refs: final_kernel(*refs, slots=slots, feeds=feeds...  2.48 us

profile of v2, /device:TPU:0, one launch (start us, length us, event | category | flops | bytes accessed | tf_op | source)
XLA Modules:
  0.0 58.5 jit_solution(7980823339279277457)
XLA Ops:
  0.6 6.2 %bin_samples.1 = (f32[32,40,128]{2,1,0:T(8,128)S(1)}, f32[256,256]{1,0:T(8,128)S(1)}, bf16[256,256]{1,0:T(8,128)(2,1)S(1)}, f32[1,256]{1,0:T(1,128)S(1)}) custom-call(s32[1]{0:T(128)} %bitcast.refs_0_, s32[8]{0:T(128)} %bitcast.16, s32[64]{0:T(128)} %refs_2_.1, s32[1,256]{1,0:T(1,128)} %bitcast.15, s32[50,256]{1,0:T(8,128)} %bitcast.12, ...), custom_call_target="tpu_custom_call" | custom-call | tf_op jit(solution)/shard_map/bin_samples/pallas_call | solution.py:403
  6.8 26.2 %all_to_all.10.refs_1_ = f32[32,40,128]{2,1,0:T(8,128)S(1)} all-to-all(f32[32,40,128]{2,1,0:T(8,128)S(1)} %get-tuple-element.12), channel_id=1, replica_groups=mesh['feed'=4,'tm'=8] {'feed','tm'}, dimensions={0} | all-to-all | bytes 1310720 | tf_op jit(solution)/shard_map/all_to_all | solution.py:429
  33.0 3.5 %solve_tiles.1 = (f32[1120,128]{1,0:T(8,128)S(1)}, f32[3,256,64]{2,1,0:T(8,128)S(1)}) custom-call(s32[1]{0:T(128)} %bitcast.refs_0_, f32[32,40,128]{2,1,0:T(8,128)S(1)} %all_to_all.10.refs_1_, f32[1,256]{1,0:T(1,128)} %bitcast.13, f32[1,256]{1,0:T(1,128)S(1)} %get-tuple-element.13.refs_3_), custom_call_target="tpu_custom_call" | custom-call | tf_op jit(solution)/shard_map/solve_tiles/pallas_call | solution.py:436
  36.5 19.4 %all_to_all.11 = f32[32,1,4480]{2,1,0:T(1,128)S(1)} all-to-all(f32[32,1,4480]{2,1,0:T(1,128)S(1)} %bitcast.10), channel_id=1, replica_groups=mesh['feed'=4,'tm'=8] {'feed','tm'}, dimensions={0} | all-to-all | bytes 1146880 | tf_op jit(solution)/shard_map/all_to_all | solution.py:453
  56.0 2.5 %finish.1 = (f32[256,256]{1,0:T(8,128)}, f32[256,256]{1,0:T(8,128)}, f32[256,64]{1,0:T(8,128)}) custom-call(f32[1120,128]{1,0:T(8,128)S(1)} %bitcast.9, f32[1,256]{1,0:T(1,128)} %bitcast.14, f32[256,256]{1,0:T(8,128)S(1)} %get-tuple-element.15.refs_2_, bf16[256,256]{1,0:T(8,128)(2,1)S(1)} %get-tuple-element.16.refs_3_, ...), custom_call_target="tpu_custom_call" | custom-call | tf_op jit(solution)/shard_map/finish/pallas_call | solution.py:456

commit v3 on v2

v3 whole, which is shorter than its diff:
```python
import functools

import jax
import jax.numpy as jnp
from jax import lax
from jax.experimental import pallas as pl
from jax.experimental.pallas import tpu as pltpu
from jax.sharding import PartitionSpec as P

CELLS = 32
EXACT = lax.Precision.HIGHEST
f32 = jnp.float32
bf16 = jnp.bfloat16


def split3(value):
    high = value.astype(bf16)
    rest = value - high.astype(f32)
    mid = rest.astype(bf16)
    low = (rest - mid.astype(f32)).astype(bf16)
    return high, mid, low


def counted(counts, value):
    out = None
    for part in split3(value):
        term = jnp.dot(counts, part, preferred_element_type=f32)
        out = term if out is None else out + term
    return out


def near(value, small):
    return pltpu.with_memory_space_constraint(value, pltpu.VMEM) if small else value


def shift_of(prior):
    return jnp.sum(prior, axis=1, keepdims=True) * (1.0 / prior.shape[1])


def pair_up(low, high):
    lane = lax.broadcasted_iota(jnp.int32, low.shape, 1)
    return jnp.where(lane < low.shape[1] // 2, low, high)


def bin_kernel(
    list_ref, place_ref, slot_ref, pix_ref, prior_ref, tod_ref,
    pay_ref, sums_ref, w_ref, power_ref, prior_out,
    tod_buf, wt_ref, t_ref, v_ref, g_ref, prior_sem, sems, *accs,
    slots, feeds, rows_owned, chunk,
):
    samples, blocks, channels = tod_ref.shape
    cells = slots * CELLS
    lanes = pay_ref.shape[2]
    width = lanes // 2
    nb = lanes // CELLS
    rb = CELLS // nb
    chunks = samples // chunk
    copies = [
        pltpu.make_async_copy(
            tod_ref.at[pl.ds(i * chunk, chunk)], tod_buf.at[pl.ds(i * chunk, chunk)], sems.at[i]
        )
        for i in range(chunks)
    ]
    for copy in copies:
        copy.start()
    extra = pltpu.make_async_copy(prior_ref, prior_out, prior_sem)
    extra.start()
    one = jnp.ones((), bf16)
    nil = jnp.zeros((), bf16)
    owner = jnp.broadcast_to(slot_ref[...], (16, blocks))
    row = lax.broadcasted_iota(jnp.int32, (16, blocks), 0)
    masks = [(owner == k).astype(f32).astype(bf16) for k in range(slots)]
    halves = [(row + q).astype(f32).astype(bf16) for q in range(0, CELLS, 16)]
    counts = [None] * len(halves)

    def hot_of(s):
        spread = jnp.broadcast_to(pix_ref[s:s + 1, :].astype(f32).astype(bf16), (16, blocks))
        hots = [jnp.where(half == spread, one, nil) for half in halves]
        for h, hot in enumerate(hots):
            counts[h] = hot if counts[h] is None else counts[h] + hot
        return jnp.concatenate([hot * masks[k] for k in range(slots) for hot in hots], axis=0)

    strips = range(0, blocks, 16)

    def add_strip(i, at):
        total = sums_ref[at:at + 16, :] if i else None
        for s in range(i * chunk, (i + 1) * chunk):
            part = tod_buf[s, at:at + 16, :].astype(f32)
            total = part if total is None else total + part
        sums_ref[at:at + 16, :] = total

    if accs:
        def push(s):
            pltpu.matmul_push_rhs(tod_buf[s], s // 2 % 2, s % 2)

        for i in range(chunks):
            copies[i].wait()
            first = i * chunk
            push(first)
            push(first + 1)
            done = 0
            for s in range(first, first + chunk):
                hot = hot_of(s)
                if s + 2 < first + chunk:
                    push(s + 2)
                pltpu.matmul_acc_lhs(accs[s % 2], hot, load_staged_rhs=s // 2 % 2)
                upto = len(strips) * (s + 1 - first) // chunk
                for at in strips[done:upto]:
                    add_strip(i, at)
                done = upto
    else:
        for i in range(chunks):
            copies[i].wait()
            first = i * chunk
            hot = jnp.concatenate([hot_of(s) for s in range(first, first + chunk)], axis=1)
            now = tod_buf[first:first + chunk].reshape(chunk * blocks, channels)
            binned = jnp.dot(hot, now, preferred_element_type=f32)
            t_ref[...] = binned if i == 0 else t_ref[...] + binned
            for at in strips:
                add_strip(i, at)

    hits = jnp.concatenate(counts, axis=0)
    wt = jnp.concatenate(
        [count * masks[k] for k in range(slots) for count in counts], axis=0
    )
    wt_ref[...] = wt
    w_ref[...] = wt.T
    sums = sums_ref[...]
    parts = split3(sums)
    if accs:
        t_ref[...] = pltpu.matmul_pop(accs[0]) + pltpu.matmul_pop(accs[1])
        every = jnp.concatenate([hits] * (cells // CELLS), axis=0)
        for n, rhs in enumerate(parts):
            pltpu.matmul_push_rhs(rhs, n // 2, n % 2)
            pltpu.matmul_acc_lhs(accs[n % 2], wt, load_staged_rhs=n // 2)
        v_ref[...] = pltpu.matmul_pop(accs[0]) + pltpu.matmul_pop(accs[1])
        pltpu.matmul_push_rhs(every, 1, 1, transpose=True)
        pltpu.matmul_acc_lhs(accs[1], wt, load_staged_rhs=1)
        g_ref[...] = pltpu.matmul_pop(accs[1])[:, 0:lanes]
    else:
        v_ref[...] = counted(wt, sums)
        every = jnp.concatenate([hits] * nb, axis=0)
        g_ref[...] = lax.dot_general(wt, every, (((1,), (1,)), ((), ())), preferred_element_type=f32)
    power_ref[...] = jnp.sum(sums * sums, axis=0, keepdims=True)
    sub = lax.broadcasted_iota(jnp.int32, (rb, lanes), 0)
    lane = lax.broadcasted_iota(jnp.int32, (rb, lanes), 1)
    mark = (sub == rb - 1) & (lane == (nb - 1) * CELLS)
    for k in range(slots):
        q0 = k * CELLS
        pack = g_ref[q0:q0 + rb, :]
        for i in range(1, nb):
            pack = jnp.where(lane >= i * CELLS, g_ref[q0 + rb * i:q0 + rb * (i + 1), :], pack)
        tile = list_ref[k]
        place = jnp.where(tile >= 0, lax.rem(place_ref[jnp.maximum(tile, 0)], rows_owned), -1)
        pack = jnp.where(mark, place.astype(f32), pack)
        for f in range(feeds):
            pay_ref[f * slots + k, CELLS:CELLS + rb, :] = pack
        for f in range(0, feeds, 2):
            binned = t_ref[q0:q0 + CELLS, f * width:(f + 2) * width]
            crossed = turn(v_ref[q0:q0 + CELLS, f * width:(f + 2) * width], width)
            pay_ref[f * slots + k, 0:CELLS, :] = pair_up(binned, crossed)
            pay_ref[(f + 1) * slots + k, 0:CELLS, :] = pair_up(crossed, binned)
    extra.wait()


def turn(value, shift):
    lanes = value.shape[1]
    shift = shift % lanes
    if shift == 0:
        return value
    if lanes % 128 == 0:
        return pltpu.roll(value, shift, 1)
    return jnp.concatenate([value[:, lanes - shift:], value[:, :lanes - shift]], axis=1)


def gram_blocks(packs):
    rb, lanes = packs[0].shape
    nb = lanes // CELLS
    lane = lax.broadcasted_iota(jnp.int32, (rb, lanes), 1)
    blocks = []
    for first in range(0, len(packs), nb):
        rows = []
        for j in range(nb):
            inside = (lane >= j * CELLS) & (lane < (j + 1) * CELLS)
            for i in range(nb):
                rows.append(jnp.where(inside, turn(packs[first + j], (j - i) * CELLS), 0.0))
        blocks.append(jnp.concatenate(rows, axis=0))
    return blocks


def stacked(block):
    return jnp.concatenate(split3(block), axis=0)


def gram_times(stack, value):
    n = stack.shape[1]
    total = None
    for j, part in enumerate(split3(value)):
        term = jnp.dot(stack[0:(3 - j) * n], part, preferred_element_type=f32)
        for i in range(3 - j):
            piece = term[i * n:(i + 1) * n]
            total = piece if total is None else total + piece
    return total


def gram_times_narrow(stack, value):
    n = stack.shape[1]
    w = value.shape[1]
    wide = jnp.dot(stack, jnp.concatenate(split3(value), axis=1), preferred_element_type=f32)
    wide = wide[2 * n:3 * n] + wide[n:2 * n] + wide[0:n]
    return wide[:, 2 * w:3 * w] + wide[:, w:2 * w] + wide[:, 0:w]


def owner_kernel(
    recv_ref, prior_ref, power_ref,
    pay_ref, map_ref,
    index_ref, even_ref, odd_ref, image_ref,
    *, feeds, rows_owned, samples, rows_out,
):
    sources, rows, lanes = recv_ref.shape
    width = lanes // 2
    nb = lanes // CELLS
    rb = CELLS // nb
    share = rb // feeds
    mark_row = CELLS + rb - 1
    mark_lane = (nb - 1) * CELLS
    feed = lax.axis_index("feed")
    flip = lax.rem(feed, 2) == 1

    def each(body):
        if sources <= 64:
            for d in range(0, sources, 2):
                body(d)
        else:
            lax.fori_loop(0, sources // 2, lambda g, c: (body(2 * g), c)[1], 0)

    def note(d):
        for e in range(2):
            at = recv_ref[d + e, mark_row:mark_row + 1, mark_lane:mark_lane + 1]
            index_ref[d + e] = jnp.max(at.astype(jnp.int32))

    def gather(d):
        for e, ref in enumerate((even_ref, odd_ref)):
            r = jnp.maximum(index_ref[d + e], 0)
            ref[r] += recv_ref[d + e]

    each(note)
    even_ref[...] = jnp.zeros(even_ref.shape, f32)
    odd_ref[...] = jnp.zeros(odd_ref.shape, f32)
    each(gather)
    sub = lax.broadcasted_iota(jnp.int32, (rb, lanes), 0)
    lane = lax.broadcasted_iota(jnp.int32, (rb, lanes), 1)
    mark = (sub == rb - 1) & (lane == mark_lane)
    packs = []
    for r in range(rows_owned):
        pack = even_ref[r, CELLS:CELLS + rb, :] + odd_ref[r, CELLS:CELLS + rb, :]
        packs.append(jnp.where(mark, pack[0:1, CELLS - 1:CELLS], pack))
    prior = prior_ref[...]
    offset = prior - shift_of(prior)
    mine = offset[:, 0:width]
    for f in range(1, feeds):
        mine = jnp.where(feed == f, offset[:, f * width:(f + 1) * width], mine)
    rr = rz = zz = zw = None
    cross = half = last = None
    for g, block in enumerate(gram_blocks(packs)):
        stack = stacked(block)
        hits = jnp.sum(block, axis=1, keepdims=True) / float(samples)
        inverse = 1.0 / jnp.maximum(hits, 1.0)
        members = range(g * nb, (g + 1) * nb)
        both = jnp.concatenate(
            [even_ref[r, 0:CELLS, :] + odd_ref[r, 0:CELLS, :] for r in members], axis=0
        )
        other = turn(both, width)
        v_sum = jnp.where(flip, both, other)[:, 0:width]
        y0 = jnp.where(flip, other, both)[:, 0:width] * inverse
        u0 = v_sum - gram_times_narrow(stack, y0)
        y1 = u0 * inverse
        uz = mine * u0 - gram_times_narrow(stack, y1)
        y2 = uz * inverse
        q0 = g * nb * CELLS
        map_ref[0, q0:q0 + nb * CELLS, :] = y0
        map_ref[1, q0:q0 + nb * CELLS, :] = y1
        map_ref[2, q0:q0 + nb * CELLS, :] = y2
        both = jnp.concatenate([jnp.where(flip, y1, y0), jnp.where(flip, y0, y1)], axis=1)
        for n, r in enumerate(members):
            image_ref[r, 0:CELLS, :] = both[n * CELLS:(n + 1) * CELLS]
        terms = [
            jnp.sum(term, axis=0, keepdims=True)
            for term in (y0 * (v_sum + u0), u0 * y1, y1 * (mine * u0 + uz), uz * y2)
        ]
        if g == 0:
            rr, cross, half, last = terms
        else:
            rr, cross, half, last = rr + terms[0], cross + terms[1], half + terms[2], last + terms[3]
    rr = -rr
    rz = mine * rr - cross
    zz = mine * mine * rr - half
    zw = mine * zz - last
    power = power_ref[...]
    parts = []
    for own in (rr, rz, zz, zw):
        for f in range(feeds):
            own = own + power[:, f * width:(f + 1) * width]
        parts.append(own[:, 0:width // 2] + own[:, width // 2:width])
        power = power * offset
    scal = jnp.concatenate(parts, axis=1)
    fill = jnp.zeros((8 - share - 1, lanes), f32)
    for r in range(rows_owned):
        quarter = packs[r][0:share]
        for f in range(1, feeds):
            quarter = jnp.where(feed == f, packs[r][f * share:(f + 1) * share], quarter)
        image_ref[r, CELLS:CELLS + 8, :] = jnp.concatenate([quarter, scal, fill], axis=0)

    def scatter(d):
        for e in range(2):
            r = jnp.maximum(index_ref[d + e], 0)
            pay_ref[pl.ds((d + e) * rows_out, rows_out), :] = image_ref[r, 0:rows_out, :]

    each(scatter)


def final_kernel(
    recv_ref, prior_ref, sums_ref, w_ref, maps_ref,
    x_out, r_out, sky_out,
    y0_ref, y1_ref, y2_ref, x_ref, r_ref, sky_ref, sems,
    *, slots, feeds, samples, share, rows_in,
):
    lanes = recv_ref.shape[1]
    sources = recv_ref.shape[0] // rows_in
    width = lanes // 2
    nb = lanes // CELLS
    prior = prior_ref[...]
    mean = shift_of(prior)
    offset = prior - mean
    sigma = mean + float(samples)
    scal = None
    for d in range(sources):
        now = recv_ref[d * rows_in + CELLS + share:d * rows_in + CELLS + share + 1, :]
        scal = now if scal is None else scal + now
    quarter = lanes // 4
    rr0, rz, zz, zw = [
        jnp.sum(scal[:, i * quarter:(i + 1) * quarter], axis=1, keepdims=True) for i in range(4)
    ]
    gamma = rz / rr0
    alpha0 = 1.0 / (sigma + gamma)
    ee = zz - gamma * rz
    rr1 = alpha0 * alpha0 * ee
    beta = rr1 / rr0
    e_a_e = sigma * ee + (zw - 2.0 * gamma * zz + gamma * gamma * rz)
    alpha1 = rr1 / (alpha0 * alpha0 * e_a_e - rr1 * beta / alpha0)
    lead = alpha0 * gamma + beta
    slack = 1.0 - alpha1 * sigma
    x_r = alpha0 + alpha1 * lead
    x_z = -alpha0 * alpha1
    r_r = alpha0 * gamma * slack - alpha1 * sigma * beta
    r_z = -alpha0 * slack - alpha1 * lead
    r_w = alpha0 * alpha1
    packs = []
    for k in range(slots):
        base = [(f * slots + k) * rows_in for f in range(feeds)]
        packs.append(
            jnp.concatenate([recv_ref[b + CELLS:b + CELLS + share, :] for b in base], axis=0)
        )
        q0 = k * CELLS
        for f in range(0, feeds, 2):
            low = recv_ref[base[f]:base[f] + CELLS, :]
            high = recv_ref[base[f + 1]:base[f + 1] + CELLS, :]
            y0_ref[q0:q0 + CELLS, f * width:(f + 2) * width] = pair_up(low, high)
            y1_ref[q0:q0 + CELLS, f * width:(f + 2) * width] = turn(pair_up(high, low), width)
    y0 = y0_ref[...]
    y1 = y1_ref[...]
    sums = sums_ref[...]
    w = w_ref[...]
    lead_x = x_r + x_z * offset
    x_ref[...] = lead_x * sums - counted(w, lead_x * y0 + x_z * y1)
    sky_ref[...] = maps_ref[0] - x_r * maps_ref[1] - x_z * maps_ref[2]
    outs = [
        pltpu.make_async_copy(x_ref, x_out, sems.at[0]),
        pltpu.make_async_copy(sky_ref, sky_out, sems.at[1]),
        pltpu.make_async_copy(r_ref, r_out, sems.at[2]),
    ]
    outs[0].start()
    outs[1].start()
    for g, block in enumerate(gram_blocks(packs)):
        stack = stacked(block)
        hits = jnp.sum(block, axis=1, keepdims=True) / float(samples)
        inverse = 1.0 / jnp.maximum(hits, 1.0)
        q0 = g * nb * CELLS
        part = y1_ref[q0:q0 + nb * CELLS, :]
        y2_ref[q0:q0 + nb * CELLS, :] = offset * part - inverse * gram_times(stack, part)
    second = r_z + r_w * offset
    lead_r = r_r + second * offset
    r_ref[...] = lead_r * sums - counted(w, lead_r * y0 + second * y1 + r_w * y2_ref[...])
    outs[2].start()
    for out in outs:
        out.wait()


def local(tod, pixels, block_slots, tile_lists, tile_place, prior):
    axes = ("feed", "tm")
    feeds = lax.axis_size("feed")
    owners = lax.axis_size("tm")
    slots = tile_lists.shape[1] * tile_lists.shape[2]
    assert slots == owners and feeds % 2 == 0
    rows_owned = tile_place.shape[0] // owners
    blocks, samples, channels = tod.shape
    cells = slots * CELLS
    width = channels // feeds
    lanes = 2 * width
    gram_rows = CELLS * CELLS // lanes
    rows = CELLS + gram_rows
    devices = feeds * owners
    chunk = max(n for n in range(1, 11) if samples % n == 0)
    small = devices * rows * lanes <= 1 << 18
    held = pltpu.VMEM if small else jax.ShapeDtypeStruct
    accs = []
    if blocks == cells == channels == 256 and chunk > 1:
        accs = [pltpu.ACC(n)((cells, channels), f32) for n in range(2)]
    smem = pl.BlockSpec(memory_space=pltpu.SMEM)
    vmem = pl.BlockSpec(memory_space=pltpu.VMEM)

    hbm = pl.BlockSpec(memory_space=pl.ANY)
    payload, sums, weights, power, prior_row = pl.pallas_call(
        lambda *refs: pl.run_scoped(
            functools.partial(
                bin_kernel, *refs, slots=slots, feeds=feeds, rows_owned=rows_owned, chunk=chunk
            ),
            *accs,
        ),
        in_specs=[smem, smem, vmem, vmem, hbm, hbm],
        out_specs=[vmem, vmem, vmem, vmem, vmem],
        out_shape=[
            held((devices, rows, lanes), f32),
            held((blocks, channels), f32),
            held((blocks, cells), bf16),
            held((1, channels), f32),
            held((1, channels), f32),
        ],
        scratch_shapes=[
            pltpu.VMEM((samples, blocks, channels), bf16),
            pltpu.VMEM((cells, blocks), bf16),
            pltpu.VMEM((cells, channels), f32),
            pltpu.VMEM((cells, channels), f32),
            pltpu.VMEM((cells, lanes), f32),
            pltpu.SemaphoreType.DMA,
            pltpu.SemaphoreType.DMA((samples // chunk,)),
        ],
        name="bin_samples",
    )(
        tile_lists.reshape(slots),
        tile_place,
        block_slots.reshape(1, blocks),
        pixels.T,
        prior.reshape(1, channels),
        tod.transpose(1, 0, 2),
    )
    received = lax.all_to_all(payload, axes, split_axis=0, concat_axis=0, tiled=True)
    owned_cells = rows_owned * CELLS
    share = gram_rows // feeds
    rows_back = CELLS + share + 1
    if not small:
        rows_back = -(-rows_back // 8) * 8
    answer, maps = pl.pallas_call(
        lambda *refs: owner_kernel(
            *refs, feeds=feeds, rows_owned=rows_owned, samples=samples, rows_out=rows_back
        ),
        in_specs=[vmem, vmem, vmem],
        out_specs=[vmem, vmem],
        out_shape=[
            held((devices * rows_back, lanes), f32),
            held((3, owned_cells, width), f32),
        ],
        scratch_shapes=[
            pltpu.SMEM((devices,), jnp.int32),
            pltpu.VMEM((rows_owned, rows, lanes), f32),
            pltpu.VMEM((rows_owned, rows, lanes), f32),
            pltpu.VMEM((rows_owned, CELLS + 8, lanes), f32),
        ],
        name="solve_tiles",
    )(near(received, small), near(prior_row, small), near(power, small))
    returned = lax.all_to_all(
        answer.reshape(devices, 1, rows_back * lanes), axes, split_axis=0, concat_axis=0, tiled=True
    ).reshape(devices * rows_back, lanes)
    drift, leftover, sky = pl.pallas_call(
        lambda *refs: final_kernel(
            *refs, slots=slots, feeds=feeds, samples=samples, share=share, rows_in=rows_back
        ),
        in_specs=[vmem, vmem, vmem, vmem, vmem],
        out_specs=[hbm, hbm, hbm],
        out_shape=[
            jax.ShapeDtypeStruct((blocks, channels), f32),
            jax.ShapeDtypeStruct((blocks, channels), f32),
            jax.ShapeDtypeStruct((owned_cells, width), f32),
        ],
        scratch_shapes=[
            pltpu.VMEM((cells, channels), f32),
            pltpu.VMEM((cells, channels), f32),
            pltpu.VMEM((cells, channels), f32),
            pltpu.VMEM((blocks, channels), f32),
            pltpu.VMEM((blocks, channels), f32),
            pltpu.VMEM((owned_cells, width), f32),
            pltpu.SemaphoreType.DMA((3,)),
        ],
        name="finish",
    )(near(returned, small), near(prior_row, small), near(sums, small), near(weights, small), near(maps, small))
    return drift, leftover, sky.reshape(rows_owned, CELLS, width)


def solution(mesh):
    return jax.shard_map(
        local,
        mesh=mesh,
        in_specs=(
            P(("feed", "tm"), None, None),
            P(("feed", "tm"), None),
            P(("feed", "tm")),
            P(("feed", "tm"), None, None),
            P(),
            P(),
        ),
        out_specs=(P(("feed", "tm"), None), P(("feed", "tm"), None), P("tm", None, "feed")),
        check_vma=False,
    )
```

time: 58.7 us -> 55.1 us (0.939)
  Pallas kernels: 12.2 us -> 8.63 us
    pallas_call x1, Pallas kernels: 3.51 us -> 1.58 us  [local(): pl.pallas_call(lambda *refs: owner_kernel(*refs, feeds=feeds, rows_owned=...]
    pallas_call x1, Pallas kernels: 6.19 us -> 5.32 us  [local(): pl.pallas_call(lambda *refs: pl.run_scoped(functools.partial(bin_kernel,...]
    pallas_call x1, Pallas kernels: 2.48 us -> 1.74 us  [local(): pl.pallas_call(lambda *refs: final_kernel(*refs, slots=slots, feeds=feeds...]
where the time goes in v3:
time: 55.1 us; the launch traced here: 54.9 us
  blocking collectives  45.6 us (83%)
  Pallas kernels  8.63 us (16%)
  between operations  0.65 us (1%)
    all_to_all x1, blocking collectives, local(): lax.all_to_all(payload, axes, split_axis=0, concat_axis=0, tiled=True)  26.2 us
    all_to_all x1, blocking collectives, local(): lax.all_to_all(answer.reshape(devices, 1, rows_back * lanes), axes, split...  19.4 us
    pallas_call x1, Pallas kernels, local(): pl.pallas_call(lambda *refs: pl.run_scoped(functools.partial(bin_kernel,...  5.32 us
    pallas_call x1, Pallas kernels, local(): pl.pallas_call(lambda *refs: final_kernel(*refs, slots=slots, feeds=feeds...  1.74 us
    pallas_call x1, Pallas kernels, local(): pl.pallas_call(lambda *refs: owner_kernel(*refs, feeds=feeds, rows_owned=...  1.58 us

profile of v3, /device:TPU:0, one launch (start us, length us, event | category | flops | bytes accessed | tf_op | source)
XLA Modules:
  0.0 54.9 jit_solution(17423522026861322281)
XLA Ops:
  0.6 5.3 %bin_samples.1 = (f32[32,40,128]{2,1,0:T(8,128)S(1)}, f32[256,256]{1,0:T(8,128)S(1)}, bf16[256,256]{1,0:T(8,128)(2,1)S(1)}, f32[1,256]{1,0:T(1,128)S(1)}, f32[1,256]{1,0:T(1,128)S(1)}) custom-call(s32[8]{0:T(128)} %bitcast.14, s32[64]{0:T(128)} %refs_1_.1, s32[1,256]{1,0:T(1,128)} %bitcast.12, s32[50,256]{1,0:T(8,128)} %bitcast.11, f32[1,256]{1,0:T(1,128)} %bitcast.13, ...), custom_call_target="tpu_custom_call" | custom-call | tf_op jit(solution)/shard_map/bin_samples/pallas_call | solution.py:423
  6.0 26.2 %all_to_all.10.refs_0_ = f32[32,40,128]{2,1,0:T(8,128)S(1)} all-to-all(f32[32,40,128]{2,1,0:T(8,128)S(1)} %get-tuple-element.13), channel_id=1, replica_groups=mesh['feed'=4,'tm'=8] {'feed','tm'}, dimensions={0} | all-to-all | bytes 1310720 | tf_op jit(solution)/shard_map/all_to_all | solution.py:457
  32.1 1.6 %solve_tiles.1 = (f32[1120,128]{1,0:T(8,128)S(1)}, f32[3,256,64]{2,1,0:T(8,128)S(1)}) custom-call(f32[32,40,128]{2,1,0:T(8,128)S(1)} %all_to_all.10.refs_0_, f32[1,256]{1,0:T(1,128)S(1)} %get-tuple-element.14.refs_1_, f32[1,256]{1,0:T(1,128)S(1)} %get-tuple-element.15.refs_2_), custom_call_target="tpu_custom_call" | custom-call | tf_op jit(solution)/shard_map/solve_tiles/pallas_call | solution.py:463
  33.7 19.4 %all_to_all.11 = f32[32,1,4480]{2,1,0:T(1,128)S(1)} all-to-all(f32[32,1,4480]{2,1,0:T(1,128)S(1)} %bitcast.9), channel_id=1, replica_groups=mesh['feed'=4,'tm'=8] {'feed','tm'}, dimensions={0} | all-to-all | bytes 1146880 | tf_op jit(solution)/shard_map/all_to_all | solution.py:481
  53.2 1.7 %finish.1 = (f32[256,256]{1,0:T(8,128)}, f32[256,256]{1,0:T(8,128)}, f32[256,64]{1,0:T(8,128)}) custom-call(f32[1120,128]{1,0:T(8,128)S(1)} %bitcast.8, f32[1,256]{1,0:T(1,128)S(1)} %get-tuple-element.14.refs_1_, f32[256,256]{1,0:T(8,128)S(1)} %get-tuple-element.17.refs_2_, bf16[256,256]{1,0:T(8,128)(2,1)S(1)} %get-tuple-element.18.refs_3_, ...), custom_call_target="tpu_custom_call" | custom-call | tf_op jit(solution)/shard_map/finish/pallas_call | solution.py:484

commit v4 on v3

--- a/solution.py
+++ b/solution.py
@@ -42,15 +42,29 @@
     return jnp.where(lane < low.shape[1] // 2, low, high)
 
 
+def mark_place(compact, rows, lanes):
+    if compact:
+        return (rows - 1, 4), (rows - 2, 5)
+    return (rows - 1, lanes - CELLS), (0, CELLS - 1)
+
+
+def mark_of(rows, lanes, compact):
+    at = mark_place(compact, rows, lanes)[0]
+    sub = lax.broadcasted_iota(jnp.int32, (rows, lanes), 0)
+    lane = lax.broadcasted_iota(jnp.int32, (rows, lanes), 1)
+    return (sub == at[0]) & (lane == at[1])
+
+
 def bin_kernel(
     list_ref, place_ref, slot_ref, pix_ref, prior_ref, tod_ref,
-    pay_ref, sums_ref, w_ref, power_ref, prior_out,
-    tod_buf, wt_ref, t_ref, v_ref, g_ref, prior_sem, sems, *accs,
-    slots, feeds, rows_owned, chunk,
+    pay_ref, sums_ref, w_ref, prior_out,
+    tod_buf, t_ref, v_ref, g_ref, prior_sem, sems, *accs,
+    slots, feeds, rows_owned, chunk, compact,
 ):
     samples, blocks, channels = tod_ref.shape
     cells = slots * CELLS
-    lanes = pay_ref.shape[2]
+    lanes = pay_ref.shape[1]
+    rows = pay_ref.shape[0] // (feeds * slots)
     width = lanes // 2
     nb = lanes // CELLS
     rb = CELLS // nb
@@ -123,8 +137,7 @@
     wt = jnp.concatenate(
         [count * masks[k] for k in range(slots) for count in counts], axis=0
     )
-    wt_ref[...] = wt
-    w_ref[...] = wt.T
+    w_ref[...] = wt
     sums = sums_ref[...]
     parts = split3(sums)
     if accs:
@@ -141,10 +154,8 @@
         v_ref[...] = counted(wt, sums)
         every = jnp.concatenate([hits] * nb, axis=0)
         g_ref[...] = lax.dot_general(wt, every, (((1,), (1,)), ((), ())), preferred_element_type=f32)
-    power_ref[...] = jnp.sum(sums * sums, axis=0, keepdims=True)
-    sub = lax.broadcasted_iota(jnp.int32, (rb, lanes), 0)
     lane = lax.broadcasted_iota(jnp.int32, (rb, lanes), 1)
-    mark = (sub == rb - 1) & (lane == (nb - 1) * CELLS)
+    mark = mark_of(rows - CELLS, lanes, compact)
     for k in range(slots):
         q0 = k * CELLS
         pack = g_ref[q0:q0 + rb, :]
@@ -152,14 +163,20 @@
             pack = jnp.where(lane >= i * CELLS, g_ref[q0 + rb * i:q0 + rb * (i + 1), :], pack)
         tile = list_ref[k]
         place = jnp.where(tile >= 0, lax.rem(place_ref[jnp.maximum(tile, 0)], rows_owned), -1)
+        if compact:
+            pack = squeeze_pack(pack)
         pack = jnp.where(mark, place.astype(f32), pack)
         for f in range(feeds):
-            pay_ref[f * slots + k, CELLS:CELLS + rb, :] = pack
+            at = (f * slots + k) * rows + CELLS
+            pay_ref[at:at + rows - CELLS, :] = pack
         for f in range(0, feeds, 2):
             binned = t_ref[q0:q0 + CELLS, f * width:(f + 2) * width]
             crossed = turn(v_ref[q0:q0 + CELLS, f * width:(f + 2) * width], width)
-            pay_ref[f * slots + k, 0:CELLS, :] = pair_up(binned, crossed)
-            pay_ref[(f + 1) * slots + k, 0:CELLS, :] = pair_up(crossed, binned)
+            for at, value in (
+                ((f * slots + k) * rows, pair_up(binned, crossed)),
+                (((f + 1) * slots + k) * rows, pair_up(crossed, binned)),
+            ):
+                pay_ref[at:at + CELLS, :] = value
     extra.wait()
 
 
@@ -173,7 +190,27 @@
     return jnp.concatenate([value[:, lanes - shift:], value[:, :lanes - shift]], axis=1)
 
 
-def gram_blocks(packs):
+def late(shape, axis):
+    return lax.rem(lax.broadcasted_iota(jnp.int32, shape, axis), 8) >= 4
+
+
+def squeeze_pack(pack):
+    low = jnp.where(late((2, 128), 1), pack[4:6], turn(pack, -4)[6:8])
+    return jnp.concatenate([pack[0:4], low], axis=0)
+
+
+def expand_pack(six):
+    low = six[4:6]
+    rest = jnp.concatenate([low, turn(low, 4)], axis=0)
+    return jnp.concatenate([six[0:4], jnp.where(late((4, 128), 1), rest, 0.0)], axis=0)
+
+
+def gram_blocks(packs, compact):
+    if compact:
+        blocks = gram_blocks([expand_pack(six) for six in packs], False)
+        shape = blocks[0].shape
+        mirror = late(shape, 1) & jnp.logical_not(late(shape, 0))
+        return [block + jnp.where(mirror, block, 0.0).T for block in blocks]
     rb, lanes = packs[0].shape
     nb = lanes // CELLS
     lane = lax.broadcasted_iota(jnp.int32, (rb, lanes), 1)
@@ -212,18 +249,19 @@
 
 
 def owner_kernel(
-    recv_ref, prior_ref, power_ref,
-    pay_ref, map_ref,
+    recv_ref, prior_ref, sums_ref, wt_ref,
+    pay_ref, map_ref, w_ref,
     index_ref, even_ref, odd_ref, image_ref,
-    *, feeds, rows_owned, samples, rows_out,
+    *, feeds, rows_owned, samples, rows, rows_out, compact,
 ):
-    sources, rows, lanes = recv_ref.shape
+    sources = recv_ref.shape[0] // rows
+    lanes = recv_ref.shape[1]
     width = lanes // 2
     nb = lanes // CELLS
     rb = CELLS // nb
     share = rb // feeds
-    mark_row = CELLS + rb - 1
-    mark_lane = (nb - 1) * CELLS
+    gram_rows = rows - CELLS
+    marked, mirrored = mark_place(compact, gram_rows, lanes)
     feed = lax.axis_index("feed")
     flip = lax.rem(feed, 2) == 1
 
@@ -236,25 +274,26 @@
 
     def note(d):
         for e in range(2):
-            at = recv_ref[d + e, mark_row:mark_row + 1, mark_lane:mark_lane + 1]
+            at = recv_ref[
+                pl.ds((d + e) * rows + CELLS + marked[0], 1), marked[1]:marked[1] + 1
+            ]
             index_ref[d + e] = jnp.max(at.astype(jnp.int32))
 
     def gather(d):
         for e, ref in enumerate((even_ref, odd_ref)):
             r = jnp.maximum(index_ref[d + e], 0)
-            ref[r] += recv_ref[d + e]
+            ref[r] += recv_ref[pl.ds((d + e) * rows, rows), :]
 
     each(note)
     even_ref[...] = jnp.zeros(even_ref.shape, f32)
     odd_ref[...] = jnp.zeros(odd_ref.shape, f32)
     each(gather)
-    sub = lax.broadcasted_iota(jnp.int32, (rb, lanes), 0)
-    lane = lax.broadcasted_iota(jnp.int32, (rb, lanes), 1)
-    mark = (sub == rb - 1) & (lane == mark_lane)
+    mark = mark_of(gram_rows, lanes, compact)
     packs = []
     for r in range(rows_owned):
-        pack = even_ref[r, CELLS:CELLS + rb, :] + odd_ref[r, CELLS:CELLS + rb, :]
-        packs.append(jnp.where(mark, pack[0:1, CELLS - 1:CELLS], pack))
+        pack = even_ref[r, CELLS:rows, :] + odd_ref[r, CELLS:rows, :]
+        mirror = pack[mirrored[0]:mirrored[0] + 1, mirrored[1]:mirrored[1] + 1]
+        packs.append(jnp.where(mark, mirror, pack))
     prior = prior_ref[...]
     offset = prior - shift_of(prior)
     mine = offset[:, 0:width]
@@ -262,7 +301,7 @@
         mine = jnp.where(feed == f, offset[:, f * width:(f + 1) * width], mine)
     rr = rz = zz = zw = None
     cross = half = last = None
-    for g, block in enumerate(gram_blocks(packs)):
+    for g, block in enumerate(gram_blocks(packs, compact)):
         stack = stacked(block)
         hits = jnp.sum(block, axis=1, keepdims=True) / float(samples)
         inverse = 1.0 / jnp.maximum(hits, 1.0)
@@ -296,16 +335,35 @@
     rz = mine * rr - cross
     zz = mine * mine * rr - half
     zw = mine * zz - last
-    power = power_ref[...]
+    sums = sums_ref[...]
+    power = jnp.sum(sums * sums, axis=0, keepdims=True)
+    w_ref[...] = wt_ref[...].T
     parts = []
     for own in (rr, rz, zz, zw):
         for f in range(feeds):
             own = own + power[:, f * width:(f + 1) * width]
-        parts.append(own[:, 0:width // 2] + own[:, width // 2:width])
+        own = own[:, 0:width // 2] + own[:, width // 2:width]
+        if compact:
+            own = own[:, 0:width // 4] + own[:, width // 4:width // 2]
+        parts.append(own)
         power = power * offset
-    scal = jnp.concatenate(parts, axis=1)
-    fill = jnp.zeros((8 - share - 1, lanes), f32)
-    for r in range(rows_owned):
+    if compact:
+        scal = jnp.concatenate(parts + parts, axis=1)
+        side = lax.broadcasted_iota(jnp.int32, (1, lanes), 1) >= width
+        keep = jnp.where(flip, side.astype(f32), 1.0 - side.astype(f32)) > 0.5
+        for r in range(rows_owned):
+            six = packs[r]
+            row = six[0:1]
+            for f in range(1, feeds):
+                row = jnp.where(feed == f, six[f:f + 1], row)
+            half_row = jnp.where(feed >= 2, six[5:6], six[4:5])
+            image_ref[r, CELLS:CELLS + 2, :] = jnp.concatenate(
+                [row, jnp.where(keep, half_row, scal)], axis=0
+            )
+    else:
+        scal = jnp.concatenate(parts, axis=1)
+        fill = jnp.zeros((8 - share - 1, lanes), f32)
+    for r in range(0 if compact else rows_owned):
         quarter = packs[r][0:share]
         for f in range(1, feeds):
             quarter = jnp.where(feed == f, packs[r][f * share:(f + 1) * share], quarter)
@@ -323,7 +381,7 @@
     recv_ref, prior_ref, sums_ref, w_ref, maps_ref,
     x_out, r_out, sky_out,
     y0_ref, y1_ref, y2_ref, x_ref, r_ref, sky_ref, sems,
-    *, slots, feeds, samples, share, rows_in,
+    *, slots, feeds, samples, share, rows_in, compact,
 ):
     lanes = recv_ref.shape[1]
     sources = recv_ref.shape[0] // rows_in
@@ -333,11 +391,14 @@
     mean = shift_of(prior)
     offset = prior - mean
     sigma = mean + float(samples)
-    scal = None
+    sides = [None, None]
     for d in range(sources):
-        now = recv_ref[d * rows_in + CELLS + share:d * rows_in + CELLS + share + 1, :]
-        scal = now if scal is None else scal + now
-    quarter = lanes // 4
+        at = d * rows_in + CELLS + share
+        side = d // slots % 2 if compact else 0
+        now = recv_ref[at:at + 1, :]
+        sides[side] = now if sides[side] is None else sides[side] + now
+    scal = sides[0][:, width:lanes] + sides[1][:, 0:width] if compact else sides[0]
+    quarter = scal.shape[1] // 4
     rr0, rz, zz, zw = [
         jnp.sum(scal[:, i * quarter:(i + 1) * quarter], axis=1, keepdims=True) for i in range(4)
     ]
@@ -358,9 +419,11 @@
     packs = []
     for k in range(slots):
         base = [(f * slots + k) * rows_in for f in range(feeds)]
-        packs.append(
-            jnp.concatenate([recv_ref[b + CELLS:b + CELLS + share, :] for b in base], axis=0)
-        )
+        pieces = [recv_ref[b + CELLS:b + CELLS + share, :] for b in base]
+        if compact:
+            ends = [recv_ref[b + CELLS + 1:b + CELLS + 2, :] for b in base]
+            pieces += [pair_up(ends[0], ends[1]), pair_up(ends[2], ends[3])]
+        packs.append(jnp.concatenate(pieces, axis=0))
         q0 = k * CELLS
         for f in range(0, feeds, 2):
             low = recv_ref[base[f]:base[f] + CELLS, :]
@@ -381,7 +444,7 @@
     ]
     outs[0].start()
     outs[1].start()
-    for g, block in enumerate(gram_blocks(packs)):
+    for g, block in enumerate(gram_blocks(packs, compact)):
         stack = stacked(block)
         hits = jnp.sum(block, axis=1, keepdims=True) / float(samples)
         inverse = 1.0 / jnp.maximum(hits, 1.0)
@@ -407,7 +470,8 @@
     cells = slots * CELLS
     width = channels // feeds
     lanes = 2 * width
-    gram_rows = CELLS * CELLS // lanes
+    compact = lanes == 128 and feeds == 4
+    gram_rows = 6 if compact else CELLS * CELLS // lanes
     rows = CELLS + gram_rows
     devices = feeds * owners
     chunk = max(n for n in range(1, 11) if samples % n == 0)
@@ -420,25 +484,24 @@
     vmem = pl.BlockSpec(memory_space=pltpu.VMEM)
 
     hbm = pl.BlockSpec(memory_space=pl.ANY)
-    payload, sums, weights, power, prior_row = pl.pallas_call(
+    payload, sums, counts, prior_row = pl.pallas_call(
         lambda *refs: pl.run_scoped(
             functools.partial(
-                bin_kernel, *refs, slots=slots, feeds=feeds, rows_owned=rows_owned, chunk=chunk
+                bin_kernel, *refs, slots=slots, feeds=feeds, rows_owned=rows_owned, chunk=chunk,
+                compact=compact,
             ),
             *accs,
         ),
         in_specs=[smem, smem, vmem, vmem, hbm, hbm],
-        out_specs=[vmem, vmem, vmem, vmem, vmem],
+        out_specs=[vmem, vmem, vmem, vmem],
         out_shape=[
-            held((devices, rows, lanes), f32),
+            held((devices * rows, lanes), f32),
             held((blocks, channels), f32),
-            held((blocks, cells), bf16),
-            held((1, channels), f32),
+            held((cells, blocks), bf16),
             held((1, channels), f32),
         ],
         scratch_shapes=[
             pltpu.VMEM((samples, blocks, channels), bf16),
-            pltpu.VMEM((cells, blocks), bf16),
             pltpu.VMEM((cells, channels), f32),
             pltpu.VMEM((cells, channels), f32),
             pltpu.VMEM((cells, lanes), f32),
@@ -454,21 +517,25 @@
         prior.reshape(1, channels),
         tod.transpose(1, 0, 2),
     )
-    received = lax.all_to_all(payload, axes, split_axis=0, concat_axis=0, tiled=True)
+    received = lax.all_to_all(
+        payload.reshape(devices, 1, rows * lanes), axes, split_axis=0, concat_axis=0, tiled=True
+    ).reshape(devices * rows, lanes)
     owned_cells = rows_owned * CELLS
-    share = gram_rows // feeds
+    share = 1 if compact else gram_rows // feeds
     rows_back = CELLS + share + 1
-    if not small:
+    if not compact:
         rows_back = -(-rows_back // 8) * 8
-    answer, maps = pl.pallas_call(
+    answer, maps, weights = pl.pallas_call(
         lambda *refs: owner_kernel(
-            *refs, feeds=feeds, rows_owned=rows_owned, samples=samples, rows_out=rows_back
+            *refs, feeds=feeds, rows_owned=rows_owned, samples=samples, rows=rows,
+            rows_out=rows_back, compact=compact
         ),
-        in_specs=[vmem, vmem, vmem],
-        out_specs=[vmem, vmem],
+        in_specs=[vmem, vmem, vmem, vmem],
+        out_specs=[vmem, vmem, vmem],
         out_shape=[
             held((devices * rows_back, lanes), f32),
             held((3, owned_cells, width), f32),
+            held((blocks, cells), bf16),
         ],
         scratch_shapes=[
             pltpu.SMEM((devices,), jnp.int32),
@@ -477,13 +544,14 @@
             pltpu.VMEM((rows_owned, CELLS + 8, lanes), f32),
         ],
         name="solve_tiles",
-    )(near(received, small), near(prior_row, small), near(power, small))
+    )(near(received, small), near(prior_row, small), near(sums, small), near(counts, small))
     returned = lax.all_to_all(
         answer.reshape(devices, 1, rows_back * lanes), axes, split_axis=0, concat_axis=0, tiled=True
     ).reshape(devices * rows_back, lanes)
     drift, leftover, sky = pl.pallas_call(
         lambda *refs: final_kernel(
-            *refs, slots=slots, feeds=feeds, samples=samples, share=share, rows_in=rows_back
+            *refs, slots=slots, feeds=feeds, samples=samples, share=share, rows_in=rows_back,
+            compact=compact,
         ),
         in_specs=[vmem, vmem, vmem, vmem, vmem],
         out_specs=[hbm, hbm, hbm],

time: 55.1 us -> 54.6 us (level)
  blocking collectives: 45.6 us -> 44.6 us
    all_to_all x1, blocking collectives: 26.2 us -> 25.5 us  [local(): lax.all_to_all(payload.reshape(devices, 1, rows * lanes), axes, split_axi...]
where the time goes in v4:
time: 54.6 us; the launch traced here: 54.4 us
  blocking collectives  44.6 us (82%)
  Pallas kernels  9.15 us (17%)
  between operations  0.65 us (1%)
    all_to_all x1, blocking collectives, local(): lax.all_to_all(payload.reshape(devices, 1, rows * lanes), axes, split_axi...  25.5 us
    all_to_all x1, blocking collectives, local(): lax.all_to_all(answer.reshape(devices, 1, rows_back * lanes), axes, split...  19.1 us
    pallas_call x1, Pallas kernels, local(): pl.pallas_call(lambda *refs: pl.run_scoped(functools.partial(bin_kernel,...  5.35 us
    pallas_call x1, Pallas kernels, local(): pl.pallas_call(lambda *refs: owner_kernel(*refs, feeds=feeds, rows_owned=...  1.97 us
    pallas_call x1, Pallas kernels, local(): pl.pallas_call(lambda *refs: final_kernel(*refs, slots=slots, feeds=feeds...  1.83 us

profile of v4, /device:TPU:0, one launch (start us, length us, event | category | flops | bytes accessed | tf_op | source)
XLA Modules:
  0.0 54.4 jit_solution(17232717769920462988)
XLA Ops:
  0.6 5.3 %bin_samples.1 = (f32[1216,128]{1,0:T(8,128)S(1)}, f32[256,256]{1,0:T(8,128)S(1)}, bf16[256,256]{1,0:T(8,128)(2,1)S(1)}, f32[1,256]{1,0:T(1,128)S(1)}) custom-call(s32[8]{0:T(128)} %bitcast.18, s32[64]{0:T(128)} %refs_1_.1, s32[1,256]{1,0:T(1,128)} %bitcast.16, s32[50,256]{1,0:T(8,128)} %bitcast.15, f32[1,256]{1,0:T(1,128)} %bitcast.17, ...), custom_call_target="tpu_custom_call" | custom-call | tf_op jit(solution)/shard_map/bin_samples/pallas_call | solution.py:487
  6.0 25.5 %all_to_all.10 = f32[32,1,4864]{2,1,0:T(1,128)S(1)} all-to-all(f32[32,1,4864]{2,1,0:T(1,128)S(1)} %bitcast.12), channel_id=1, replica_groups=mesh['feed'=4,'tm'=8] {'feed','tm'}, dimensions={0} | all-to-all | bytes 1245184 | tf_op jit(solution)/shard_map/all_to_all | solution.py:520
  31.5 2.0 %solve_tiles.1 = (f32[1088,128]{1,0:T(8,128)S(1)}, f32[3,256,64]{2,1,0:T(8,128)S(1)}, bf16[256,256]{1,0:T(8,128)(2,1)S(1)}) custom-call(f32[1216,128]{1,0:T(8,128)S(1)} %bitcast.10, f32[1,256]{1,0:T(1,128)S(1)} %get-tuple-element.14.refs_1_, f32[256,256]{1,0:T(8,128)S(1)} %get-tuple-element.15.refs_2_, bf16[256,256]{1,0:T(8,128)(2,1)S(1)} %get-tuple-element.16.refs_3_), custom_call_target="tpu_custom_call" | custom-call | tf_op jit(solution)/shard_map/solve_tiles/pallas_call | solution.py:528
  33.4 19.1 %all_to_all.11 = f32[32,1,4352]{2,1,0:T(1,128)S(1)} all-to-all(f32[32,1,4352]{2,1,0:T(1,128)S(1)} %bitcast.13), channel_id=1, replica_groups=mesh['feed'=4,'tm'=8] {'feed','tm'}, dimensions={0} | all-to-all | bytes 1114112 | tf_op jit(solution)/shard_map/all_to_all | solution.py:548
  52.5 1.8 %finish.1 = (f32[256,256]{1,0:T(8,128)}, f32[256,256]{1,0:T(8,128)}, f32[256,64]{1,0:T(8,128)}) custom-call(f32[1088,128]{1,0:T(8,128)S(1)} %bitcast.11, f32[1,256]{1,0:T(1,128)S(1)} %get-tuple-element.14.refs_1_, f32[256,256]{1,0:T(8,128)S(1)} %get-tuple-element.15.refs_2_, bf16[256,256]{1,0:T(8,128)(2,1)S(1)} %get-tuple-element.18.refs_3_, ...), custom_call_target="tpu_custom_call" | custom-call | tf_op jit(solution)/shard_map/finish/pallas_call | solution.py:551

commit v5 on v4

--- a/solution.py
+++ b/solution.py
@@ -141,15 +141,15 @@
     sums = sums_ref[...]
     parts = split3(sums)
     if accs:
-        t_ref[...] = pltpu.matmul_pop(accs[0]) + pltpu.matmul_pop(accs[1])
         every = jnp.concatenate([hits] * (cells // CELLS), axis=0)
+        pltpu.matmul_push_rhs(every, 1, 1, transpose=True)
+        pltpu.matmul_acc_lhs(accs[4], wt, load_staged_rhs=1)
         for n, rhs in enumerate(parts):
             pltpu.matmul_push_rhs(rhs, n // 2, n % 2)
-            pltpu.matmul_acc_lhs(accs[n % 2], wt, load_staged_rhs=n // 2)
-        v_ref[...] = pltpu.matmul_pop(accs[0]) + pltpu.matmul_pop(accs[1])
-        pltpu.matmul_push_rhs(every, 1, 1, transpose=True)
-        pltpu.matmul_acc_lhs(accs[1], wt, load_staged_rhs=1)
-        g_ref[...] = pltpu.matmul_pop(accs[1])[:, 0:lanes]
+            pltpu.matmul_acc_lhs(accs[2 + n % 2], wt, load_staged_rhs=n // 2)
+        t_ref[...] = pltpu.matmul_pop(accs[0]) + pltpu.matmul_pop(accs[1])
+        g_ref[...] = pltpu.matmul_pop(accs[4])[:, 0:lanes]
+        v_ref[...] = pltpu.matmul_pop(accs[2]) + pltpu.matmul_pop(accs[3])
     else:
         v_ref[...] = counted(wt, sums)
         every = jnp.concatenate([hits] * nb, axis=0)
@@ -479,7 +479,7 @@
     held = pltpu.VMEM if small else jax.ShapeDtypeStruct
     accs = []
     if blocks == cells == channels == 256 and chunk > 1:
-        accs = [pltpu.ACC(n)((cells, channels), f32) for n in range(2)]
+        accs = [pltpu.ACC(n)((cells, channels), f32) for n in (0, 1, 0, 1, 1)]
     smem = pl.BlockSpec(memory_space=pltpu.SMEM)
     vmem = pl.BlockSpec(memory_space=pltpu.VMEM)
 

time: 54.6 us -> 54.5 us (level)
  no operation moved by 1% of the time
where the time goes in v5:
time: 54.5 us; the launch traced here: 54.3 us
  blocking collectives  44.6 us (82%)
  Pallas kernels  9.04 us (17%)
  between operations  0.65 us (1%)
    all_to_all x1, blocking collectives, local(): lax.all_to_all(payload.reshape(devices, 1, rows * lanes), axes, split_axi...  25.5 us
    all_to_all x1, blocking collectives, local(): lax.all_to_all(answer.reshape(devices, 1, rows_back * lanes), axes, split...  19.1 us
    pallas_call x1, Pallas kernels, local(): pl.pallas_call(lambda *refs: pl.run_scoped(functools.partial(bin_kernel,...  5.23 us
    pallas_call x1, Pallas kernels, local(): pl.pallas_call(lambda *refs: owner_kernel(*refs, feeds=feeds, rows_owned=...  1.97 us
    pallas_call x1, Pallas kernels, local(): pl.pallas_call(lambda *refs: final_kernel(*refs, slots=slots, feeds=feeds...  1.83 us

profile of v5, /device:TPU:0, one launch (start us, length us, event | category | flops | bytes accessed | tf_op | source)
XLA Modules:
  0.0 54.3 jit_solution(14834371722305501880)
XLA Ops:
  0.6 5.2 %bin_samples.1 = (f32[1216,128]{1,0:T(8,128)S(1)}, f32[256,256]{1,0:T(8,128)S(1)}, bf16[256,256]{1,0:T(8,128)(2,1)S(1)}, f32[1,256]{1,0:T(1,128)S(1)}) custom-call(s32[8]{0:T(128)} %bitcast.18, s32[64]{0:T(128)} %refs_1_.1, s32[1,256]{1,0:T(1,128)} %bitcast.16, s32[50,256]{1,0:T(8,128)} %bitcast.15, f32[1,256]{1,0:T(1,128)} %bitcast.17, ...), custom_call_target="tpu_custom_call" | custom-call | tf_op jit(solution)/shard_map/bin_samples/pallas_call | solution.py:487
  5.9 25.5 %all_to_all.10 = f32[32,1,4864]{2,1,0:T(1,128)S(1)} all-to-all(f32[32,1,4864]{2,1,0:T(1,128)S(1)} %bitcast.12), channel_id=1, replica_groups=mesh['feed'=4,'tm'=8] {'feed','tm'}, dimensions={0} | all-to-all | bytes 1245184 | tf_op jit(solution)/shard_map/all_to_all | solution.py:520
  31.4 2.0 %solve_tiles.1 = (f32[1088,128]{1,0:T(8,128)S(1)}, f32[3,256,64]{2,1,0:T(8,128)S(1)}, bf16[256,256]{1,0:T(8,128)(2,1)S(1)}) custom-call(f32[1216,128]{1,0:T(8,128)S(1)} %bitcast.10, f32[1,256]{1,0:T(1,128)S(1)} %get-tuple-element.14.refs_1_, f32[256,256]{1,0:T(8,128)S(1)} %get-tuple-element.15.refs_2_, bf16[256,256]{1,0:T(8,128)(2,1)S(1)} %get-tuple-element.16.refs_3_), custom_call_target="tpu_custom_call" | custom-call | tf_op jit(solution)/shard_map/solve_tiles/pallas_call | solution.py:528
  33.3 19.1 %all_to_all.11 = f32[32,1,4352]{2,1,0:T(1,128)S(1)} all-to-all(f32[32,1,4352]{2,1,0:T(1,128)S(1)} %bitcast.13), channel_id=1, replica_groups=mesh['feed'=4,'tm'=8] {'feed','tm'}, dimensions={0} | all-to-all | bytes 1114112 | tf_op jit(solution)/shard_map/all_to_all | solution.py:548
  52.4 1.8 %finish.1 = (f32[256,256]{1,0:T(8,128)}, f32[256,256]{1,0:T(8,128)}, f32[256,64]{1,0:T(8,128)}) custom-call(f32[1088,128]{1,0:T(8,128)S(1)} %bitcast.11, f32[1,256]{1,0:T(1,128)S(1)} %get-tuple-element.14.refs_1_, f32[256,256]{1,0:T(8,128)S(1)} %get-tuple-element.15.refs_2_, bf16[256,256]{1,0:T(8,128)(2,1)S(1)} %get-tuple-element.18.refs_3_, ...), custom_call_target="tpu_custom_call" | custom-call | tf_op jit(solution)/shard_map/finish/pallas_call | solution.py:551

commit v6 on v5

--- a/solution.py
+++ b/solution.py
@@ -251,9 +251,10 @@
 def owner_kernel(
     recv_ref, prior_ref, sums_ref, wt_ref,
     pay_ref, map_ref, w_ref,
-    index_ref, even_ref, odd_ref, image_ref,
-    *, feeds, rows_owned, samples, rows, rows_out, compact,
+    index_ref, *banks,
+    feeds, rows_owned, samples, rows, rows_out, compact,
 ):
+    *banks, image_ref = banks
     sources = recv_ref.shape[0] // rows
     lanes = recv_ref.shape[1]
     width = lanes // 2
@@ -267,31 +268,35 @@
 
     def each(body):
         if sources <= 64:
-            for d in range(0, sources, 2):
+            for d in range(0, sources, 4):
                 body(d)
         else:
-            lax.fori_loop(0, sources // 2, lambda g, c: (body(2 * g), c)[1], 0)
+            lax.fori_loop(0, sources // 4, lambda g, c: (body(4 * g), c)[1], 0)
 
     def note(d):
-        for e in range(2):
+        for e in range(4):
             at = recv_ref[
                 pl.ds((d + e) * rows + CELLS + marked[0], 1), marked[1]:marked[1] + 1
             ]
             index_ref[d + e] = jnp.max(at.astype(jnp.int32))
 
     def gather(d):
-        for e, ref in enumerate((even_ref, odd_ref)):
+        for e, ref in enumerate(banks):
             r = jnp.maximum(index_ref[d + e], 0)
             ref[r] += recv_ref[pl.ds((d + e) * rows, rows), :]
 
+    def gathered(r, first, last):
+        a, b, c, e = [ref[r, first:last, :] for ref in banks]
+        return (a + b) + (c + e)
+
     each(note)
-    even_ref[...] = jnp.zeros(even_ref.shape, f32)
-    odd_ref[...] = jnp.zeros(odd_ref.shape, f32)
+    for ref in banks:
+        ref[...] = jnp.zeros(ref.shape, f32)
     each(gather)
     mark = mark_of(gram_rows, lanes, compact)
     packs = []
     for r in range(rows_owned):
-        pack = even_ref[r, CELLS:rows, :] + odd_ref[r, CELLS:rows, :]
+        pack = gathered(r, CELLS, rows)
         mirror = pack[mirrored[0]:mirrored[0] + 1, mirrored[1]:mirrored[1] + 1]
         packs.append(jnp.where(mark, mirror, pack))
     prior = prior_ref[...]
@@ -307,7 +312,7 @@
         inverse = 1.0 / jnp.maximum(hits, 1.0)
         members = range(g * nb, (g + 1) * nb)
         both = jnp.concatenate(
-            [even_ref[r, 0:CELLS, :] + odd_ref[r, 0:CELLS, :] for r in members], axis=0
+            [gathered(r, 0, CELLS) for r in members], axis=0
         )
         other = turn(both, width)
         v_sum = jnp.where(flip, both, other)[:, 0:width]
@@ -370,7 +375,7 @@
         image_ref[r, CELLS:CELLS + 8, :] = jnp.concatenate([quarter, scal, fill], axis=0)
 
     def scatter(d):
-        for e in range(2):
+        for e in range(4):
             r = jnp.maximum(index_ref[d + e], 0)
             pay_ref[pl.ds((d + e) * rows_out, rows_out), :] = image_ref[r, 0:rows_out, :]
 
@@ -464,7 +469,7 @@
     feeds = lax.axis_size("feed")
     owners = lax.axis_size("tm")
     slots = tile_lists.shape[1] * tile_lists.shape[2]
-    assert slots == owners and feeds % 2 == 0
+    assert slots == owners and feeds % 4 == 0
     rows_owned = tile_place.shape[0] // owners
     blocks, samples, channels = tod.shape
     cells = slots * CELLS
@@ -539,8 +544,7 @@
         ],
         scratch_shapes=[
             pltpu.SMEM((devices,), jnp.int32),
-            pltpu.VMEM((rows_owned, rows, lanes), f32),
-            pltpu.VMEM((rows_owned, rows, lanes), f32),
+            *[pltpu.VMEM((rows_owned, rows, lanes), f32) for _ in range(4)],
             pltpu.VMEM((rows_owned, CELLS + 8, lanes), f32),
         ],
         name="solve_tiles",

time: 54.5 us -> 54.5 us (level)
  no operation moved by 1% of the time
where the time goes in v6:
time: 54.5 us; the launch traced here: 54.2 us
  blocking collectives  44.6 us (82%)
  Pallas kernels  9.02 us (17%)
  between operations  0.65 us (1%)
    all_to_all x1, blocking collectives, local(): lax.all_to_all(payload.reshape(devices, 1, rows * lanes), axes, split_axi...  25.5 us
    all_to_all x1, blocking collectives, local(): lax.all_to_all(answer.reshape(devices, 1, rows_back * lanes), axes, split...  19.1 us
    pallas_call x1, Pallas kernels, local(): pl.pallas_call(lambda *refs: pl.run_scoped(functools.partial(bin_kernel,...  5.23 us
    pallas_call x1, Pallas kernels, local(): pl.pallas_call(lambda *refs: owner_kernel(*refs, feeds=feeds, rows_owned=...  1.96 us
    pallas_call x1, Pallas kernels, local(): pl.pallas_call(lambda *refs: final_kernel(*refs, slots=slots, feeds=feeds...  1.83 us

profile of v6, /device:TPU:0, one launch (start us, length us, event | category | flops | bytes accessed | tf_op | source)
XLA Modules:
  0.0 54.2 jit_solution(16574394321295238092)
XLA Ops:
  0.6 5.2 %bin_samples.1 = (f32[1216,128]{1,0:T(8,128)S(1)}, f32[256,256]{1,0:T(8,128)S(1)}, bf16[256,256]{1,0:T(8,128)(2,1)S(1)}, f32[1,256]{1,0:T(1,128)S(1)}) custom-call(s32[8]{0:T(128)} %bitcast.18, s32[64]{0:T(128)} %refs_1_.1, s32[1,256]{1,0:T(1,128)} %bitcast.16, s32[50,256]{1,0:T(8,128)} %bitcast.15, f32[1,256]{1,0:T(1,128)} %bitcast.17, ...), custom_call_target="tpu_custom_call" | custom-call | tf_op jit(solution)/shard_map/bin_samples/pallas_call | solution.py:492
  5.9 25.5 %all_to_all.10 = f32[32,1,4864]{2,1,0:T(1,128)S(1)} all-to-all(f32[32,1,4864]{2,1,0:T(1,128)S(1)} %bitcast.12), channel_id=1, replica_groups=mesh['feed'=4,'tm'=8] {'feed','tm'}, dimensions={0} | all-to-all | bytes 1245184 | tf_op jit(solution)/shard_map/all_to_all | solution.py:525
  31.4 2.0 %solve_tiles.1 = (f32[1088,128]{1,0:T(8,128)S(1)}, f32[3,256,64]{2,1,0:T(8,128)S(1)}, bf16[256,256]{1,0:T(8,128)(2,1)S(1)}) custom-call(f32[1216,128]{1,0:T(8,128)S(1)} %bitcast.10, f32[1,256]{1,0:T(1,128)S(1)} %get-tuple-element.14.refs_1_, f32[256,256]{1,0:T(8,128)S(1)} %get-tuple-element.15.refs_2_, bf16[256,256]{1,0:T(8,128)(2,1)S(1)} %get-tuple-element.16.refs_3_), custom_call_target="tpu_custom_call" | custom-call | tf_op jit(solution)/shard_map/solve_tiles/pallas_call | solution.py:533
  33.3 19.1 %all_to_all.11 = f32[32,1,4352]{2,1,0:T(1,128)S(1)} all-to-all(f32[32,1,4352]{2,1,0:T(1,128)S(1)} %bitcast.13), channel_id=1, replica_groups=mesh['feed'=4,'tm'=8] {'feed','tm'}, dimensions={0} | all-to-all | bytes 1114112 | tf_op jit(solution)/shard_map/all_to_all | solution.py:552
  52.4 1.8 %finish.1 = (f32[256,256]{1,0:T(8,128)}, f32[256,256]{1,0:T(8,128)}, f32[256,64]{1,0:T(8,128)}) custom-call(f32[1088,128]{1,0:T(8,128)S(1)} %bitcast.11, f32[1,256]{1,0:T(1,128)S(1)} %get-tuple-element.14.refs_1_, f32[256,256]{1,0:T(8,128)S(1)} %get-tuple-element.15.refs_2_, bf16[256,256]{1,0:T(8,128)(2,1)S(1)} %get-tuple-element.18.refs_3_, ...), custom_call_target="tpu_custom_call" | custom-call | tf_op jit(solution)/shard_map/finish/pallas_call | solution.py:555
